TPU v7x, 512 devices: a whole 4x8x8 slice. The times are simulated.
512 devices in a mesh: sec: 2 (over x_hi), wide: 128 (over z, x_lo, y), grp: 2 (over core).
Axes of the slice: x: 4 (x_hi: 2, x_lo: 2; x = x_hi * 2 + x_lo), y: 8, z: 8, core: 2. Of those that a mesh axis runs over, the one named last changes fastest.
Arguments:
- embeddings: bfloat16 [2, 131072, 1024], P('sec', ('wide', 'grp'))
- bin_ids: int32 [512], replicated, may hold values from 2 to 511, as said below
- positives: int32 [131072], P(('wide', 'grp')), may hold values from 0 to 131071, as said below
Outputs:
- grads: bfloat16 [2, 131072, 1024], P('sec', ('wide', 'grp'))
Inputs may be any that keep to these rules, and one draw needn't show every extreme that they name: `bin_ids`: bin ids never fall from one block to the next; each id covers 1 to 3 consecutive blocks, the first id covers 3, and the last block's id is 511. positives maps the spectrum rows of each bin one to one onto the molecule rows of the same bin.
All inputs are finite; a program needn't handle non-finite values.
Results may differ from a plain program's by a relative error of at most 0.01.
Values may be sent and summed in bfloat16 or wider, within the bound.
A program may use at most 64 MiB of HBM per device.

v0:
```python
import jax
import jax.numpy as jnp
from jax import lax
from jax.sharding import PartitionSpec as P

BLOCK = 256


logit_scale = 0.125
reach_blocks = 2


def swapped(value, axis, apart):
    mask = 2**apart
    pairs = [(source, source ^ mask) for source in range(lax.axis_size(axis))]
    return lax.ppermute(value, axis, pairs)


def with_halo(block, sides, width):
    for axis, dim in sides:
        count = lax.axis_size(axis)
        forward = [(i, i + 1) for i in range(count - 1)]
        backward = [(target, source) for source, target in forward]
        low = lax.ppermute(
            lax.slice_in_dim(block, block.shape[dim] - width, None, axis=dim), axis, forward
        )
        high = lax.ppermute(lax.slice_in_dim(block, 0, width, axis=dim), axis, backward)
        block = jnp.concatenate([low, block, high], axis=dim)
    return block


def from_behind(array, axis, by):
    devices = lax.axis_size(axis)
    pairs = [(i, i + by) for i in range(devices) if 0 <= i + by < devices]
    return lax.ppermute(array, axis, pairs)


def local(embeddings, bin_ids, positives):
    own_rows = embeddings[0]
    row_count = own_rows.shape[0]
    features = own_rows.shape[1]
    blocks = row_count // BLOCK
    first_block = lax.axis_index(("wide", "grp")) * blocks
    section = lax.axis_index("sec")
    spectral = (section == 0).astype(jnp.float32)
    partner = swapped(embeddings, "sec", 0)
    shaped = partner.reshape(blocks, BLOCK, features)
    beside_all = with_halo(shaped, ((("wide", "grp"), 0),), reach_blocks)
    key_rows = beside_all.reshape((blocks + 2 * reach_blocks) * BLOCK, features)
    padded_bins = jnp.pad(bin_ids, reach_blocks, constant_values=-1)
    near_bins = lax.dynamic_slice_in_dim(padded_bins, first_block, blocks + 2 * reach_blocks, 0)
    own_bins = lax.dynamic_slice_in_dim(bin_ids, first_block, blocks, 0)
    allowed = jnp.repeat(own_bins, BLOCK)[:, None] == jnp.repeat(near_bins, BLOCK)[None, :]
    scores = logit_scale * lax.dot_general(
        own_rows, key_rows, (((1,), (1,)), ((), ())), preferred_element_type=jnp.float32
    )
    scores = jnp.where(allowed, scores, -jnp.inf)
    row_top = jnp.max(scores, axis=1, keepdims=True)
    totals = jnp.log(jnp.sum(jnp.exp(scores - row_top), axis=1, keepdims=True)) + row_top
    columns = (first_block - reach_blocks) * BLOCK + jnp.arange(key_rows.shape[0], dtype=jnp.int32)
    target_hits = (columns[None, :] == positives[:, None]).astype(jnp.float32)
    weights = (jnp.exp(scores - totals) - 2.0 * spectral * target_hits).astype(jnp.bfloat16)
    query_grad = logit_scale * jnp.dot(weights, key_rows, preferred_element_type=jnp.float32)
    key_terms = logit_scale * lax.dot_general(
        weights, own_rows, (((0,), (0,)), ((), ())), preferred_element_type=jnp.float32
    )
    key_terms = key_terms.reshape(blocks + 2 * reach_blocks, BLOCK, features)
    from_right = from_behind(key_terms[:reach_blocks], ("wide", "grp"), -1)
    from_left = from_behind(key_terms[reach_blocks + blocks :], ("wide", "grp"), 1)
    mine_terms = key_terms[reach_blocks : reach_blocks + blocks]
    mine_terms = mine_terms.at[blocks - reach_blocks :].add(from_right)
    mine_terms = mine_terms.at[:reach_blocks].add(from_left)
    returned = swapped(mine_terms.reshape(row_count, features), "sec", 0)
    total_grad = query_grad + returned
    return total_grad.astype(jnp.bfloat16)[None]


def solution(mesh):
    in_specs = (P("sec", ("wide", "grp"), None), P(), P(("wide", "grp")))
    out_specs = P("sec", ("wide", "grp"), None)
    return jax.shard_map(local, mesh=mesh, in_specs=in_specs, out_specs=out_specs, check_vma=False)
```

profile of v0, /device:TPU:249, one launch (start us, length us, event | category | flops | bytes accessed | tf_op | source)
XLA Modules:
  0.0 143.8 jit_solution(149079255551198503)
XLA Ops:
  0.0 4.6 %collective-permute-start = (bf16[1,512,1024]{2,1,0:T(8,128)(2,1)}, bf16[1,512,1024]{2,1,0:T(8,128)(2,1)S(1)}, u32[]{:S(2)}, u32[]{:S(2)}) collective-permute-start(bf16[1,512,1024]{2,1,0:T(8,128)(2,1)} %param.11), channel_id=1, source_target_pairs={{0,256},{256,0},{1,257},{257,1},{2,258},{258,2},{3,259},{259,3},{4... | collective-permute-start | bytes 3145736 | tf_op jit(solution)/shard_map/ppermute | solution.py:16
  4.7 23.0 %collective-permute-done = bf16[1,512,1024]{2,1,0:T(8,128)(2,1)S(1)} collective-permute-done((bf16[1,512,1024]{2,1,0:T(8,128)(2,1)}, bf16[1,512,1024]{2,1,0:T(8,128)(2,1)S(1)}, u32[]{:S(2)}, u32[]{:S(2)}) %collective-permute-start) | collective-permute-done | bytes 1048608 | tf_op jit(solution)/shard_map/ppermute | solution.py:16
  27.6 3.4 %collective-permute-start.2 = (bf16[2,256,1024]{2,1,0:T(8,128)(2,1)S(1)}, bf16[2,256,1024]{2,1,0:T(8,128)(2,1)S(1)}, u32[]{:S(2)}, u32[]{:S(2)}) collective-permute-start(bf16[2,256,1024]{2,1,0:T(8,128)(2,1)S(1)} %bitcast.30), channel_id=1, source_target_pairs={{1,0},{2,1},{3,2},{4,3},{5,4},{6,5},{7,6},{8,7},{9,8},{10,9},{11,1... | collective-permute-start | bytes 3145736 | tf_op jit(solution)/shard_map/ppermute | solution.py:27
  31.1 4.2 %collective-permute-start.1 = (bf16[2,256,1024]{2,1,0:T(8,128)(2,1)S(1)}, bf16[2,256,1024]{2,1,0:T(8,128)(2,1)S(1)}, u32[]{:S(2)}, u32[]{:S(2)}) collective-permute-start(bf16[2,256,1024]{2,1,0:T(8,128)(2,1)S(1)} %bitcast.31), channel_id=1, source_target_pairs={{0,1},{1,2},{2,3},{3,4},{4,5},{5,6},{6,7},{7,8},{8,9},{9,10},{10,1... | collective-permute-start | bytes 3145736 | tf_op jit(solution)/shard_map/ppermute | solution.py:24
  35.3 0.8 dynamic_slice.6
  36.1 0.1 broadcast_bitcast_fusion
  36.2 0.8 pad_dynamic-slice_fusion
  37.0 8.8 %collective-permute-done.2 = bf16[2,256,1024]{2,1,0:T(8,128)(2,1)S(1)} collective-permute-done((bf16[2,256,1024]{2,1,0:T(8,128)(2,1)S(1)}, bf16[2,256,1024]{2,1,0:T(8,128)(2,1)S(1)}, u32[]{:S(2)}, u32[]{:S(2)}) %collective-permute-start.2) | collective-permute-done | bytes 1048608 | tf_op jit(solution)/shard_map/ppermute | solution.py:27
  45.8 1.2 collective-permute-done.1
  47.0 0.4 pad_maximum_fusion
  47.4 2.0 %fusion.8 = (f32[512]{0:T(512)S(1)}, f32[512,1536]{0,1:T(8,128)S(1)}) fusion(bf16[1536,1024]{1,0:T(8,128)(2,1)S(1)} %bitcast.26, bf16[1,512,1024]{2,1,0:T(8,128)(2,1)S(1)} %copy-done, s32[1536]{0:T(1024)S(1)} %eq.35, s32[512]{0:T(512)S(1)} %bitcast.33), kind=kOutput, calls=%fused_computation.19 | convolution fusion | flops 1613757952 | bytes 7350272 | tf_op jit(solution)/shard_map/dot_general | solution.py:54
  49.4 0.5 exponential_reduce_fusion
  50.0 0.2 copy-done.1
  50.1 2.0 %convolution_multiply_fusion = f32[1536,1024]{1,0:T(8,128)S(1)} fusion(bf16[1,512,1024]{2,1,0:T(8,128)(2,1)S(1)} %copy-done, f32[512,1536]{0,1:T(8,128)S(1)} %get-tuple-element.48, f32[]{:T(128)S(6)} %mul_shard_map.3, s32[512]{0:T(512)S(1)} %copy-done.1, f32[512]{0:T(512)S(1)} %log_add_fusion, s32[1536]{0:T(1024)S(1)} %iota_add_fusion), kind=kOutput, calls=%fused_computation | convolution fusion | flops 1616117760 | bytes 10496004 | tf_op jit(solution)/shard_map/dot_general | solution.py:64
  52.1 0.6 fusion.7
  52.7 6.5 %collective-permute-start.4 = (f32[2,256,1024]{2,1,0:T(8,128)S(1)}, f32[2,256,1024]{2,1,0:T(8,128)S(1)}, u32[]{:S(2)}, u32[]{:S(2)}) collective-permute-start(f32[2,256,1024]{2,1,0:T(8,128)S(1)} %bitcast.29), channel_id=1, source_target_pairs={{0,1},{1,2},{2,3},{3,4},{4,5},{5,6},{6,7},{7,8},{8,9},{9,10},{10,1... | collective-permute-start | bytes 6291464 | tf_op jit(solution)/shard_map/ppermute | solution.py:35
  59.2 1.9 %collective-permute-start.3 = (f32[2,256,1024]{2,1,0:T(8,128)S(1)}, f32[2,256,1024]{2,1,0:T(8,128)S(1)}, u32[]{:S(2)}, u32[]{:S(2)}) collective-permute-start(f32[2,256,1024]{2,1,0:T(8,128)S(1)} %bitcast.28), channel_id=1, source_target_pairs={{1,0},{2,1},{3,2},{4,3},{5,4},{6,5},{7,6},{8,7},{9,8},{10,9},{11,1... | collective-permute-start | bytes 6291464 | tf_op jit(solution)/shard_map/ppermute | solution.py:35
  61.2 21.0 %collective-permute-done.4 = f32[2,256,1024]{2,1,0:T(8,128)S(1)} collective-permute-done((f32[2,256,1024]{2,1,0:T(8,128)S(1)}, f32[2,256,1024]{2,1,0:T(8,128)S(1)}, u32[]{:S(2)}, u32[]{:S(2)}) %collective-permute-start.4) | collective-permute-done | bytes 2097184 | tf_op jit(solution)/shard_map/ppermute | solution.py:35
  82.2 6.5 %collective-permute-done.3 = f32[2,256,1024]{2,1,0:T(8,128)S(1)} collective-permute-done((f32[2,256,1024]{2,1,0:T(8,128)S(1)}, f32[2,256,1024]{2,1,0:T(8,128)S(1)}, u32[]{:S(2)}, u32[]{:S(2)}) %collective-permute-start.3) | collective-permute-done | bytes 2097184 | tf_op jit(solution)/shard_map/ppermute | solution.py:35
  88.7 0.8 fusion.2
  89.6 4.6 %collective-permute-start.5 = (f32[512,1024]{1,0:T(8,128)S(1)}, f32[512,1024]{1,0:T(8,128)S(1)}, u32[]{:S(2)}, u32[]{:S(2)}) collective-permute-start(f32[512,1024]{1,0:T(8,128)S(1)} %fusion.2), channel_id=1, source_target_pairs={{0,256},{256,0},{1,257},{257,1},{2,258},{258,2},{3,259},{259,3},{4... | collective-permute-start | bytes 6291464 | tf_op jit(solution)/shard_map/ppermute | solution.py:16
  94.2 1.9 %fusion.6 = f32[512,1024]{1,0:T(8,128)S(1)} fusion(bf16[1536,1024]{1,0:T(8,128)(2,1)S(1)} %bitcast.27, f32[512,1536]{0,1:T(8,128)S(1)} %get-tuple-element.48, f32[]{:T(128)S(6)} %mul_shard_map.3, s32[512]{0:T(512)S(1)} %copy-done.1, f32[512]{0:T(512)S(1)} %log_add_fusion, s32[1536]{0:T(1024)S(1)} %iota_add_fusion), kind=kOutput, calls=%fused_computation.17 | convolution fusion | flops 1614544896 | bytes 8398852 | tf_op jit(solution)/shard_map/dot_general | solution.py:63
  96.1 46.2 %collective-permute-done.5 = f32[512,1024]{1,0:T(8,128)S(1)} collective-permute-done((f32[512,1024]{1,0:T(8,128)S(1)}, f32[512,1024]{1,0:T(8,128)S(1)}, u32[]{:S(2)}, u32[]{:S(2)}) %collective-permute-start.5) | collective-permute-done | bytes 2097184 | tf_op jit(solution)/shard_map/ppermute | solution.py:16
  142.4 1.5 %fusion.3 = bf16[1,512,1024]{2,1,0:T(8,128)(2,1)} fusion(f32[512,1024]{1,0:T(8,128)S(1)} %collective-permute-done.5, f32[512,1024]{1,0:T(8,128)S(1)} %fusion.6), kind=kLoop, calls=%fused_computation.10 | loop fusion | flops 1572864 | bytes 5242880 | tf_op jit(solution)/shard_map/broadcast_in_dim | solution.py:75
  (8 shorter events, 0.1 us)
Async XLA Ops:
  0.0 27.6 %collective-permute-start = (bf16[1,512,1024]{2,1,0:T(8,128)(2,1)}, bf16[1,512,1024]{2,1,0:T(8,128)(2,1)S(1)}, u32[]{:S(2)}, u32[]{:S(2)}) collective-permute-start(bf16[1,512,1024]{2,1,0:T(8,128)(2,1)} %param.11), channel_id=1, source_target_pairs={{0,256},{256,0},{1,257},{257,1},{2,258},{258,2},{3,259},{259,3},{4... | collective-permute-start | bytes 3145736 | tf_op jit(solution)/shard_map/ppermute | solution.py:16
  27.6 18.2 %collective-permute-start.2 = (bf16[2,256,1024]{2,1,0:T(8,128)(2,1)S(1)}, bf16[2,256,1024]{2,1,0:T(8,128)(2,1)S(1)}, u32[]{:S(2)}, u32[]{:S(2)}) collective-permute-start(bf16[2,256,1024]{2,1,0:T(8,128)(2,1)S(1)} %bitcast.30), channel_id=1, source_target_pairs={{1,0},{2,1},{3,2},{4,3},{5,4},{6,5},{7,6},{8,7},{9,8},{10,9},{11,1... | collective-permute-start | bytes 3145736 | tf_op jit(solution)/shard_map/ppermute | solution.py:27
  31.1 15.9 %collective-permute-start.1 = (bf16[2,256,1024]{2,1,0:T(8,128)(2,1)S(1)}, bf16[2,256,1024]{2,1,0:T(8,128)(2,1)S(1)}, u32[]{:S(2)}, u32[]{:S(2)}) collective-permute-start(bf16[2,256,1024]{2,1,0:T(8,128)(2,1)S(1)} %bitcast.31), channel_id=1, source_target_pairs={{0,1},{1,2},{2,3},{3,4},{4,5},{5,6},{6,7},{7,8},{8,9},{9,10},{10,1... | collective-permute-start | bytes 3145736 | tf_op jit(solution)/shard_map/ppermute | solution.py:24
  37.0 10.4 %copy-start = (bf16[1,512,1024]{2,1,0:T(8,128)(2,1)S(1)}, bf16[1,512,1024]{2,1,0:T(8,128)(2,1)}, u32[]{:S(2)}) copy-start(bf16[1,512,1024]{2,1,0:T(8,128)(2,1)} %param.11) | copy-start | bytes 3145732
  49.4 0.7 copy-start.1
  52.7 29.5 %collective-permute-start.4 = (f32[2,256,1024]{2,1,0:T(8,128)S(1)}, f32[2,256,1024]{2,1,0:T(8,128)S(1)}, u32[]{:S(2)}, u32[]{:S(2)}) collective-permute-start(f32[2,256,1024]{2,1,0:T(8,128)S(1)} %bitcast.29), channel_id=1, source_target_pairs={{0,1},{1,2},{2,3},{3,4},{4,5},{5,6},{6,7},{7,8},{8,9},{9,10},{10,1... | collective-permute-start | bytes 6291464 | tf_op jit(solution)/shard_map/ppermute | solution.py:35
  59.2 29.5 %collective-permute-start.3 = (f32[2,256,1024]{2,1,0:T(8,128)S(1)}, f32[2,256,1024]{2,1,0:T(8,128)S(1)}, u32[]{:S(2)}, u32[]{:S(2)}) collective-permute-start(f32[2,256,1024]{2,1,0:T(8,128)S(1)} %bitcast.28), channel_id=1, source_target_pairs={{1,0},{2,1},{3,2},{4,3},{5,4},{6,5},{7,6},{8,7},{9,8},{10,9},{11,1... | collective-permute-start | bytes 6291464 | tf_op jit(solution)/shard_map/ppermute | solution.py:35
  89.6 52.8 %collective-permute-start.5 = (f32[512,1024]{1,0:T(8,128)S(1)}, f32[512,1024]{1,0:T(8,128)S(1)}, u32[]{:S(2)}, u32[]{:S(2)}) collective-permute-start(f32[512,1024]{1,0:T(8,128)S(1)} %fusion.2), channel_id=1, source_target_pairs={{0,256},{256,0},{1,257},{257,1},{2,258},{258,2},{3,259},{259,3},{4... | collective-permute-start | bytes 6291464 | tf_op jit(solution)/shard_map/ppermute | solution.py:16
where the time goes:
time: 144 us
  waiting for transfers between devices  107 us (74%)
  starting transfers between devices  25.4 us (18%)
  matrix products  5.97 us (4%)
  other arithmetic  3.21 us (2%)
  local copies, waits for them, and re-layouts  2.42 us (2%)
    ppermute x2, waiting for transfers between devices, swapped(): return lax.ppermute(value, axis, pairs)  69.2 us
    ppermute x2, waiting for transfers between devices, from_behind(): return lax.ppermute(array, axis, pairs)  27.5 us
    ppermute x2, starting transfers between devices, swapped(): return lax.ppermute(value, axis, pairs)  9.28 us
    ppermute x1, waiting for transfers between devices, with_halo(): lax.ppermute(lax.slice_in_dim(block, 0, width, axis=dim), axis, backward)  8.85 us
    ppermute x2, starting transfers between devices, from_behind(): return lax.ppermute(array, axis, pairs)  8.42 us
    ppermute x1, starting transfers between devices, with_halo(): lax.ppermute(lax.slice_in_dim(block, block.shape[dim] - width, None, axis...  4.22 us
    ppermute x1, starting transfers between devices, with_halo(): lax.ppermute(lax.slice_in_dim(block, 0, width, axis=dim), axis, backward)  3.44 us
  transfers between devices with their start and end apart: 6, of which 6 were waited for; matrix products, arithmetic and copies ran while one was open for 3% of the time, Pallas kernels for 0%

commit v1 on v0

v1 whole, which is shorter than its diff:
```python
import jax
import jax.numpy as jnp
from jax import lax
from jax.sharding import PartitionSpec as P

BLOCK = 256
logit_scale = 0.125
ROWS = ("wide", "grp")


def swapped(value, axis):
    pairs = [(source, source ^ 1) for source in range(lax.axis_size(axis))]
    return lax.ppermute(value, axis, pairs)


def neighbours(value, axis):
    count = lax.axis_size(axis)
    forward = [(i, i + 1) for i in range(count - 1)]
    backward = [(i + 1, i) for i in range(count - 1)]
    from_left = lax.ppermute(value, axis, forward)
    from_right = lax.ppermute(value, axis, backward)
    return from_left, from_right


def masked_lse(scores, allowed, axis):
    top = jnp.max(jnp.where(allowed, scores, -jnp.inf), axis=axis, keepdims=True)
    top = jnp.where(jnp.isfinite(top), top, 0.0)
    total = jnp.sum(jnp.where(allowed, jnp.exp(scores - top), 0.0), axis=axis, keepdims=True)
    return jnp.log(total) + top


def local(embeddings, bin_ids, positives):
    own = embeddings[0]
    row_count, features = own.shape
    blocks = row_count // BLOCK
    me = lax.axis_index(ROWS)
    first_row = me * row_count
    spectral = lax.axis_index("sec") == 0

    partner = swapped(own, "sec")
    own_left, own_right = neighbours(own, ROWS)
    pos_left, pos_right = neighbours(positives, ROWS)
    partner_left, partner_right = neighbours(partner, ROWS)

    own_win = jnp.concatenate([own_left, own, own_right], axis=0)
    partner_win = jnp.concatenate([partner_left, partner, partner_right], axis=0)
    pos_win = jnp.concatenate([pos_left, positives, pos_right], axis=0)
    win = 3 * row_count

    padded = jnp.pad(bin_ids, blocks, constant_values=-1)
    near_bins = lax.dynamic_slice_in_dim(padded, me * blocks, 3 * blocks, 0)
    row_bins = jnp.repeat(near_bins, BLOCK)
    own_bins = jnp.where(row_bins < 0, -1, row_bins)
    partner_bins = jnp.where(row_bins < 0, -2, row_bins)
    allowed = own_bins[:, None] == partner_bins[None, :]

    scores = logit_scale * lax.dot_general(
        own_win, partner_win, (((1,), (1,)), ((), ())), preferred_element_type=jnp.float32
    )
    partner_total = masked_lse(scores, allowed, 0)
    mine = slice(row_count, 2 * row_count)
    own_scores = scores[mine]
    own_allowed = allowed[mine]
    own_total = masked_lse(own_scores, own_allowed, 1)

    window_index = first_row - row_count + jnp.arange(win, dtype=jnp.int32)
    own_index = first_row + jnp.arange(row_count, dtype=jnp.int32)
    spectra_hits = window_index[None, :] == positives[:, None]
    molecule_hits = pos_win[None, :] == own_index[:, None]
    hits = jnp.where(spectral, spectra_hits, molecule_hits).astype(jnp.float32)

    weights = jnp.exp(own_scores - own_total) + jnp.exp(own_scores - partner_total)
    weights = jnp.where(own_allowed, weights, 0.0) - 2.0 * hits
    grad = logit_scale * jnp.dot(
        weights.astype(jnp.bfloat16), partner_win, preferred_element_type=jnp.float32
    )
    return grad.astype(jnp.bfloat16)[None]


def solution(mesh):
    in_specs = (P("sec", ROWS, None), P(), P(ROWS))
    out_specs = P("sec", ROWS, None)
    return jax.shard_map(local, mesh=mesh, in_specs=in_specs, out_specs=out_specs, check_vma=False)
```

time: 144 us -> 85.4 us (0.59)
  the two profiles are of different devices: /device:TPU:249 before, /device:TPU:255 now
where the time goes in v1:
time: 85.4 us; the launch traced here: 85.1 us
  waiting for transfers between devices  35.5 us (42%)
  starting transfers between devices  27.4 us (32%)
  matrix products  12.3 us (14%)
  other arithmetic  6.15 us (7%)
  local copies, waits for them, and re-layouts  3.6 us (4%)
    ppermute x1, waiting for transfers between devices, swapped(): return lax.ppermute(value, axis, pairs)  20.5 us
    ppermute x3, starting transfers between devices, neighbours(): from_left = lax.ppermute(value, axis, forward)  18.6 us
    ppermute x3, waiting for transfers between devices, neighbours(): from_right = lax.ppermute(value, axis, backward)  14.9 us
    dot_general x1, matrix products, local(): lax.dot_general(own_win, partner_win, (((1,), (1,)), ((), ())), preferred...  7.84 us
    ppermute x3, starting transfers between devices, neighbours(): from_right = lax.ppermute(value, axis, backward)  5.77 us
    dot_general x1, matrix products, local(): jnp.dot(weights.astype(jnp.bfloat16), partner_win, preferred_element_type...  4.42 us
    reduce_sum x2, other arithmetic, masked_lse(): jnp.sum(jnp.where(allowed, jnp.exp(scores - top), 0.0), axis=axis, keepdi...  3.19 us
    ppermute x1, starting transfers between devices, swapped(): return lax.ppermute(value, axis, pairs)  3.02 us
  transfers between devices with their start and end apart: 7, of which 2 were waited for; matrix products, arithmetic and copies ran while one was open for 7% of the time, Pallas kernels for 0%

profile of v1, /device:TPU:255, one launch (start us, length us, event | category | flops | bytes accessed | tf_op | source)
XLA Modules:
  0.0 85.1 jit_solution(3752764325072599852)
XLA Ops:
  0.0 3.0 %collective-permute-start.2 = (bf16[512,1024]{1,0:T(8,128)(2,1)}, bf16[512,1024]{1,0:T(8,128)(2,1)S(1)}, u32[]{:S(2)}, u32[]{:S(2)}) collective-permute-start(bf16[512,1024]{1,0:T(8,128)(2,1)} %bitcast.5), channel_id=1, source_target_pairs={{0,256},{256,0},{1,257},{257,1},{2,258},{258,2},{3,259},{259,3},{4... | collective-permute-start | bytes 3145736 | tf_op jit(solution)/shard_map/ppermute | solution.py:13
  3.0 4.6 %collective-permute-start = (bf16[512,1024]{1,0:T(8,128)(2,1)}, bf16[512,1024]{1,0:T(8,128)(2,1)}, u32[]{:S(2)}, u32[]{:S(2)}) collective-permute-start(bf16[512,1024]{1,0:T(8,128)(2,1)} %bitcast.6), channel_id=1, source_target_pairs={{0,1},{1,2},{2,3},{3,4},{4,5},{5,6},{6,7},{7,8},{8,9},{9,10},{10,1... | collective-permute-start | bytes 3145736 | tf_op jit(solution)/shard_map/ppermute | solution.py:20
  7.7 1.9 %collective-permute-start.1 = (bf16[512,1024]{1,0:T(8,128)(2,1)}, bf16[512,1024]{1,0:T(8,128)(2,1)}, u32[]{:S(2)}, u32[]{:S(2)}) collective-permute-start(bf16[512,1024]{1,0:T(8,128)(2,1)} %bitcast.7), channel_id=1, source_target_pairs={{1,0},{2,1},{3,2},{4,3},{5,4},{6,5},{7,6},{8,7},{9,8},{10,9},{11,1... | collective-permute-start | bytes 3145736 | tf_op jit(solution)/shard_map/ppermute | solution.py:21
  9.6 7.9 %collective-permute-start.5 = (s32[512]{0:T(512)}, s32[512]{0:T(512)S(1)}, u32[]{:S(2)}, u32[]{:S(2)}) collective-permute-start(s32[512]{0:T(512)} %param.5), channel_id=1, source_target_pairs={{0,1},{1,2},{2,3},{3,4},{4,5},{5,6},{6,7},{7,8},{8,9},{9,10},{10,1... | collective-permute-start | bytes 6152 | tf_op jit(solution)/shard_map/ppermute | solution.py:20
  17.5 0.8 pad_dynamic-slice_fusion
  18.2 0.1 broadcast_in_dim.46
  18.3 20.5 %collective-permute-done.2 = bf16[512,1024]{1,0:T(8,128)(2,1)S(1)} collective-permute-done((bf16[512,1024]{1,0:T(8,128)(2,1)}, bf16[512,1024]{1,0:T(8,128)(2,1)S(1)}, u32[]{:S(2)}, u32[]{:S(2)}) %collective-permute-start.2) | collective-permute-done | bytes 1048608 | tf_op jit(solution)/shard_map/ppermute | solution.py:13
  38.9 6.1 %collective-permute-start.3 = (bf16[512,1024]{1,0:T(8,128)(2,1)S(1)}, bf16[512,1024]{1,0:T(8,128)(2,1)}, u32[]{:S(2)}, u32[]{:S(2)}) collective-permute-start(bf16[512,1024]{1,0:T(8,128)(2,1)S(1)} %collective-permute-done.2), channel_id=1, source_target_pairs={{0,1},{1,2},{2,3},{3,4},{4,5},{5,6},{6,7},{7,8},{8,9},{9,10},{10,1... | collective-permute-start | bytes 3145736 | tf_op jit(solution)/shard_map/ppermute | solution.py:20
  45.0 1.9 %collective-permute-start.4 = (bf16[512,1024]{1,0:T(8,128)(2,1)S(1)}, bf16[512,1024]{1,0:T(8,128)(2,1)}, u32[]{:S(2)}, u32[]{:S(2)}) collective-permute-start(bf16[512,1024]{1,0:T(8,128)(2,1)S(1)} %collective-permute-done.2), channel_id=1, source_target_pairs={{1,0},{2,1},{3,2},{4,3},{5,4},{6,5},{7,6},{8,7},{9,8},{10,9},{11,1... | collective-permute-start | bytes 3145736 | tf_op jit(solution)/shard_map/ppermute | solution.py:21
  46.9 1.6 %broadcast_compare_fusion = pred[1536,1536]{1,0:T(32,128)(4,1)S(1)} fusion(s32[1536]{0:T(1024)S(1)} %get-tuple-element.6, s32[1536]{0:T(1024)S(1)} %get-tuple-element.5), kind=kLoop, calls=%fused_computation.3 | loop fusion | flops 2359296 | bytes 2371584 | tf_op jit(solution)/shard_map/eq | solution.py:55
  48.6 1.9 %collective-permute-start.6 = (s32[512]{0:T(512)}, s32[512]{0:T(512)S(1)}, u32[]{:S(2)}, u32[]{:S(2)}) collective-permute-start(s32[512]{0:T(512)} %param.5), channel_id=1, source_target_pairs={{1,0},{2,1},{3,2},{4,3},{5,4},{6,5},{7,6},{8,7},{9,8},{10,9},{11,1... | collective-permute-start | bytes 6152 | tf_op jit(solution)/shard_map/ppermute | solution.py:21
  50.5 14.9 %collective-permute-done.6 = s32[512]{0:T(512)S(1)} collective-permute-done((s32[512]{0:T(512)}, s32[512]{0:T(512)S(1)}, u32[]{:S(2)}, u32[]{:S(2)}) %collective-permute-start.6) | collective-permute-done | bytes 2080 | tf_op jit(solution)/shard_map/ppermute | solution.py:21
  65.4 0.7 pad_add_fusion
  66.1 0.0 collective-permute-done.3
  66.1 1.4 %constant_dynamic-update-slice_fusion.2 = bf16[1536,1024]{1,0:T(8,128)(2,1)S(1)} fusion(bf16[512,1024]{1,0:T(8,128)(2,1)} %collective-permute-done.3), kind=kLoop, calls=%fused_computation.27 | loop fusion | bytes 2097152
  67.5 0.1 constant_dynamic-update-slice_fusion.1
  67.6 0.0 collective-permute-done.4
  67.6 1.3 %constant_dynamic-update-slice_fusion = bf16[1536,1024]{1,0:T(8,128)(2,1)S(1)} fusion(bf16[1536,1024]{1,0:T(8,128)(2,1)S(1)} %constant_dynamic-update-slice_fusion.1, bf16[512,1024]{1,0:T(8,128)(2,1)} %collective-permute-done.4), kind=kLoop, calls=%fused_computation.25 | loop fusion | bytes 2097152 | tf_op jit(solution)/shard_map/concatenate | solution.py:46
  68.9 7.8 %select_reduce_fusion.1 = (f32[1536]{0:T(1024)S(1)}, f32[1536,1536]{1,0:T(8,128)S(1)}) fusion(s32[1536]{0:T(1024)S(1)} %get-tuple-element.6, s32[1536]{0:T(1024)S(1)} %get-tuple-element.5, bf16[1536,1024]{1,0:T(8,128)(2,1)S(1)} %constant_dynamic-update-slice_fusion, bf16[512,1024]{1,0:T(8,128)(2,1)} %collective-permute-done.1, ...), kind=kOutput, calls=%fused_computation.2 | convolution fusion | flops 4850711040 | bytes 15747072 | tf_op jit(solution)/shard_map/dot_general | solution.py:57
  76.8 0.6 select_reduce_fusion.3
  77.4 0.9 %select_reduce_fusion.2 = f32[512]{0:T(512)S(1)} fusion(f32[1536,1536]{1,0:T(8,128)S(1)} %get-tuple-element.8, pred[1536,1536]{1,0:T(32,128)(4,1)S(1)} %broadcast_compare_fusion, f32[512]{0:T(512)S(1)} %is-finite_select_fusion.1), kind=kLoop, calls=%fused_computation.10 | loop fusion | flops 2358784 | bytes 3936256 | tf_op jit(solution)/shard_map/reduce_sum | solution.py:28
  78.3 0.0 copy-start
  78.3 2.3 %select_reduce_fusion = f32[1536]{0:T(1024)S(1)} fusion(f32[1536,1536]{1,0:T(8,128)S(1)} %get-tuple-element.8, f32[1536]{0:T(1024)S(1)} %is-finite_select_fusion, s32[1536]{0:T(1024)S(1)} %get-tuple-element.6, s32[1536]{0:T(1024)S(1)} %get-tuple-element.5), kind=kLoop, calls=%fused_computation.1 | loop fusion | flops 9435648 | bytes 9461760 | tf_op jit(solution)/shard_map/reduce_sum | solution.py:28
  80.6 4.4 %fusion.13 = bf16[1,512,1024]{2,1,0:T(8,128)(2,1)} fusion(bf16[1536,1024]{1,0:T(8,128)(2,1)S(1)} %constant_dynamic-update-slice_fusion, f32[1536,1536]{1,0:T(8,128)S(1)} %get-tuple-element.8, pred[1536,1536]{1,0:T(32,128)(4,1)S(1)} %broadcast_compare_fusion, s32[1536]{0:T(1024)S(1)} %pad_add_fusion, s32[1536]{0:T(1024)S(1)} %iota_add_fusion, ...), kind=kOutput, calls=%fused_computation.21 | convolution fusion | flops 1619525632 | bytes 8157185 | tf_op jit(solution)/shard_map/dot_general | solution.py:74
  (14 shorter events, 0.1 us)
Async XLA Ops:
  0.0 38.9 %collective-permute-start.2 = (bf16[512,1024]{1,0:T(8,128)(2,1)}, bf16[512,1024]{1,0:T(8,128)(2,1)S(1)}, u32[]{:S(2)}, u32[]{:S(2)}) collective-permute-start(bf16[512,1024]{1,0:T(8,128)(2,1)} %bitcast.5), channel_id=1, source_target_pairs={{0,256},{256,0},{1,257},{257,1},{2,258},{258,2},{3,259},{259,3},{4... | collective-permute-start | bytes 3145736 | tf_op jit(solution)/shard_map/ppermute | solution.py:13
  3.0 65.9 %collective-permute-start = (bf16[512,1024]{1,0:T(8,128)(2,1)}, bf16[512,1024]{1,0:T(8,128)(2,1)}, u32[]{:S(2)}, u32[]{:S(2)}) collective-permute-start(bf16[512,1024]{1,0:T(8,128)(2,1)} %bitcast.6), channel_id=1, source_target_pairs={{0,1},{1,2},{2,3},{3,4},{4,5},{5,6},{6,7},{7,8},{8,9},{9,10},{10,1... | collective-permute-start | bytes 3145736 | tf_op jit(solution)/shard_map/ppermute | solution.py:20
  7.7 61.3 %collective-permute-start.1 = (bf16[512,1024]{1,0:T(8,128)(2,1)}, bf16[512,1024]{1,0:T(8,128)(2,1)}, u32[]{:S(2)}, u32[]{:S(2)}) collective-permute-start(bf16[512,1024]{1,0:T(8,128)(2,1)} %bitcast.7), channel_id=1, source_target_pairs={{1,0},{2,1},{3,2},{4,3},{5,4},{6,5},{7,6},{8,7},{9,8},{10,9},{11,1... | collective-permute-start | bytes 3145736 | tf_op jit(solution)/shard_map/ppermute | solution.py:21
  9.6 39.0 %collective-permute-start.5 = (s32[512]{0:T(512)}, s32[512]{0:T(512)S(1)}, u32[]{:S(2)}, u32[]{:S(2)}) collective-permute-start(s32[512]{0:T(512)} %param.5), channel_id=1, source_target_pairs={{0,1},{1,2},{2,3},{3,4},{4,5},{5,6},{6,7},{7,8},{8,9},{9,10},{10,1... | collective-permute-start | bytes 6152 | tf_op jit(solution)/shard_map/ppermute | solution.py:20
  38.9 27.3 %collective-permute-start.3 = (bf16[512,1024]{1,0:T(8,128)(2,1)S(1)}, bf16[512,1024]{1,0:T(8,128)(2,1)}, u32[]{:S(2)}, u32[]{:S(2)}) collective-permute-start(bf16[512,1024]{1,0:T(8,128)(2,1)S(1)} %collective-permute-done.2), channel_id=1, source_target_pairs={{0,1},{1,2},{2,3},{3,4},{4,5},{5,6},{6,7},{7,8},{8,9},{9,10},{10,1... | collective-permute-start | bytes 3145736 | tf_op jit(solution)/shard_map/ppermute | solution.py:20
  45.0 22.6 %collective-permute-start.4 = (bf16[512,1024]{1,0:T(8,128)(2,1)S(1)}, bf16[512,1024]{1,0:T(8,128)(2,1)}, u32[]{:S(2)}, u32[]{:S(2)}) collective-permute-start(bf16[512,1024]{1,0:T(8,128)(2,1)S(1)} %collective-permute-done.2), channel_id=1, source_target_pairs={{1,0},{2,1},{3,2},{4,3},{5,4},{6,5},{7,6},{8,7},{9,8},{10,9},{11,1... | collective-permute-start | bytes 3145736 | tf_op jit(solution)/shard_map/ppermute | solution.py:21
  48.6 16.9 %collective-permute-start.6 = (s32[512]{0:T(512)}, s32[512]{0:T(512)S(1)}, u32[]{:S(2)}, u32[]{:S(2)}) collective-permute-start(s32[512]{0:T(512)} %param.5), channel_id=1, source_target_pairs={{1,0},{2,1},{3,2},{4,3},{5,4},{6,5},{7,6},{8,7},{9,8},{10,9},{11,1... | collective-permute-start | bytes 6152 | tf_op jit(solution)/shard_map/ppermute | solution.py:21
  66.1 2.8 %copy-start.1 = (bf16[1,512,1024]{2,1,0:T(8,128)(2,1)S(1)}, bf16[1,512,1024]{2,1,0:T(8,128)(2,1)}, u32[]{:S(2)}) copy-start(bf16[1,512,1024]{2,1,0:T(8,128)(2,1)} %param.3) | copy-start | bytes 3145732
  78.3 2.3 %copy-start = (s32[512]{0:T(512)S(1)}, s32[512]{0:T(512)}, u32[]{:S(2)}) copy-start(s32[512]{0:T(512)} %param.5) | copy-start | bytes 6148

commit v2 on v1

--- a/solution.py
+++ b/solution.py
@@ -1,6 +1,10 @@
+import functools
+
 import jax
 import jax.numpy as jnp
 from jax import lax
+from jax.experimental import pallas as pl
+from jax.experimental.pallas import tpu as pltpu
 from jax.sharding import PartitionSpec as P
 
 BLOCK = 256
@@ -22,6 +26,131 @@
     return from_left, from_right
 
 
+MESH_ID = pl.DeviceIdType.MESH
+CHUNKS = 4
+
+
+def exchange_kernel(groups, own_ref, zeros_ref, own_win, partner_win, local_sem,
+                    sec_send, sec_recv, fwd_send, fwd_recv, halo_send, halo_recv):
+    rows = own_ref.shape[0]
+    piece = rows // CHUNKS
+    sec = lax.axis_index("sec")
+    wide = lax.axis_index("wide")
+    grp = lax.axis_index("grp")
+    count = lax.axis_size("wide") * groups
+    me = wide * groups + grp
+    has_left = me > 0
+    has_right = me < count - 1
+    partner_id = (1 - sec, wide, grp)
+    left_id = (sec, (me - 1) // groups, (me - 1) % groups)
+    right_id = (sec, (me + 1) // groups, (me + 1) % groups)
+
+    barrier = pltpu.get_barrier_semaphore()
+    pl.semaphore_signal(barrier, 1, device_id=partner_id, device_id_type=MESH_ID)
+
+    @pl.when(has_left)
+    def _():
+        pl.semaphore_signal(barrier, 1, device_id=left_id, device_id_type=MESH_ID)
+
+    @pl.when(has_right)
+    def _():
+        pl.semaphore_signal(barrier, 1, device_id=right_id, device_id_type=MESH_ID)
+
+    peers = 1 + has_left.astype(jnp.int32) + has_right.astype(jnp.int32)
+    pl.semaphore_wait(barrier, peers)
+
+    def sec_copy(c):
+        return pltpu.make_async_remote_copy(
+            src_ref=own_ref.at[pl.ds(c * piece, piece)],
+            dst_ref=partner_win.at[pl.ds(rows + c * piece, piece)],
+            send_sem=sec_send.at[c], recv_sem=sec_recv.at[c],
+            device_id=partner_id, device_id_type=MESH_ID)
+
+    def halo_copy(d):
+        return pltpu.make_async_remote_copy(
+            src_ref=own_ref,
+            dst_ref=own_win.at[pl.ds((1 - d) * 2 * rows, rows)],
+            send_sem=halo_send.at[d], recv_sem=halo_recv.at[d],
+            device_id=left_id if d == 0 else right_id, device_id_type=MESH_ID)
+
+    def fwd_copy(d, c):
+        return pltpu.make_async_remote_copy(
+            src_ref=partner_win.at[pl.ds(rows + c * piece, piece)],
+            dst_ref=partner_win.at[pl.ds((1 - d) * 2 * rows + c * piece, piece)],
+            send_sem=fwd_send.at[d, c], recv_sem=fwd_recv.at[d, c],
+            device_id=left_id if d == 0 else right_id, device_id_type=MESH_ID)
+
+    for c in range(CHUNKS):
+        sec_copy(c).start()
+    sides = ((0, has_left), (1, has_right))
+    for d, present in sides:
+        @pl.when(present)
+        def _():
+            halo_copy(d).start()
+
+    centre = pltpu.make_async_copy(own_ref, own_win.at[pl.ds(rows, rows)], local_sem.at[0])
+    centre.start()
+
+    for c in range(CHUNKS):
+        sec_copy(c).wait_recv()
+        for d, present in sides:
+            @pl.when(present)
+            def _():
+                fwd_copy(d, c).start()
+
+    for d, present in sides:
+        @pl.when(present)
+        def _():
+            halo_copy(d).wait_send()
+            for c in range(CHUNKS):
+                fwd_copy(d, c).wait_send()
+
+        arrived = has_right if d == 0 else has_left
+
+        @pl.when(arrived)
+        def _():
+            halo_copy(d).wait_recv()
+            for c in range(CHUNKS):
+                fwd_copy(d, c).wait_recv()
+
+    for c in range(CHUNKS):
+        sec_copy(c).wait_send()
+    centre.wait()
+
+    for d, arrived in ((0, has_right), (1, has_left)):
+        @pl.when(jnp.logical_not(arrived))
+        def _():
+            place = pl.ds((1 - d) * 2 * rows, rows)
+            first = pltpu.make_async_copy(zeros_ref, own_win.at[place], local_sem.at[1])
+            second = pltpu.make_async_copy(zeros_ref, partner_win.at[place], local_sem.at[2])
+            first.start()
+            second.start()
+            first.wait()
+            second.wait()
+
+
+def exchange(own, groups):
+    rows, features = own.shape
+    window = jax.ShapeDtypeStruct((3 * rows, features), own.dtype)
+    anywhere = pl.BlockSpec(memory_space=pl.ANY)
+    return pl.pallas_call(
+        functools.partial(exchange_kernel, groups),
+        out_shape=(window, window),
+        in_specs=[anywhere, anywhere],
+        out_specs=(anywhere, anywhere),
+        scratch_shapes=[
+            pltpu.SemaphoreType.DMA((3,)),
+            pltpu.SemaphoreType.DMA((CHUNKS,)),
+            pltpu.SemaphoreType.DMA((CHUNKS,)),
+            pltpu.SemaphoreType.DMA((2, CHUNKS)),
+            pltpu.SemaphoreType.DMA((2, CHUNKS)),
+            pltpu.SemaphoreType.DMA((2,)),
+            pltpu.SemaphoreType.DMA((2,)),
+        ],
+        compiler_params=pltpu.CompilerParams(collective_id=0, has_side_effects=True),
+    )(own, jnp.zeros_like(own))
+
+
 def masked_lse(scores, allowed, axis):
     top = jnp.max(jnp.where(allowed, scores, -jnp.inf), axis=axis, keepdims=True)
     top = jnp.where(jnp.isfinite(top), top, 0.0)
@@ -37,13 +166,8 @@
     first_row = me * row_count
     spectral = lax.axis_index("sec") == 0
 
-    partner = swapped(own, "sec")
-    own_left, own_right = neighbours(own, ROWS)
+    own_win, partner_win = exchange(own, lax.axis_size("grp"))
     pos_left, pos_right = neighbours(positives, ROWS)
-    partner_left, partner_right = neighbours(partner, ROWS)
-
-    own_win = jnp.concatenate([own_left, own, own_right], axis=0)
-    partner_win = jnp.concatenate([partner_left, partner, partner_right], axis=0)
     pos_win = jnp.concatenate([pos_left, positives, pos_right], axis=0)
     win = 3 * row_count
 

time: 85.4 us -> 145 us (1.70)
  the two profiles are of different devices: /device:TPU:255 before, /device:TPU:4 now
where the time goes in v2:
time: 145 us
  Pallas kernels  117 us (81%)
  matrix products  15.3 us (11%)
  other arithmetic  5.49 us (4%)
  local copies, waits for them, and re-layouts  3.99 us (3%)
  starting transfers between devices  3.02 us (2%)
    pallas_call x1, Pallas kernels, exchange(): pl.pallas_call(functools.partial(exchange_kernel, groups), out_shape=(win...  117 us
    dot_general x1, matrix products, local(): lax.dot_general(own_win, partner_win, (((1,), (1,)), ((), ())), preferred...  8.48 us
    dot_general x1, matrix products, local(): jnp.dot(weights.astype(jnp.bfloat16), partner_win, preferred_element_type...  6.87 us
    reduce_sum x2, other arithmetic, masked_lse(): jnp.sum(jnp.where(allowed, jnp.exp(scores - top), 0.0), axis=axis, keepdi...  3.18 us
  transfers between devices with their start and end apart: 2, of which 0 were waited for; matrix products, arithmetic and copies ran while one was open for 11% of the time, Pallas kernels for 81%

profile of v2, /device:TPU:4, one launch (start us, length us, event | category | flops | bytes accessed | tf_op | source)
XLA Modules:
  0.0 145.0 jit_solution(5414178446651886136)
XLA Ops:
  0.0 1.7 %collective-permute-start = (s32[512]{0:T(512)}, s32[512]{0:T(512)S(1)}, u32[]{:S(2)}, u32[]{:S(2)}) collective-permute-start(s32[512]{0:T(512)} %param.5), channel_id=1, source_target_pairs={{0,1},{1,2},{2,3},{3,4},{4,5},{5,6},{6,7},{7,8},{8,9},{9,10},{10,1... | collective-permute-start | bytes 6152 | tf_op jit(solution)/shard_map/ppermute | solution.py:24
  1.7 1.3 collective-permute-start.1
  3.0 0.8 pad_dynamic-slice_fusion
  3.8 0.1 broadcast_in_dim.49
  3.9 1.1 broadcast_in_dim.52.zeros_ref
  5.0 117.0 %shard_map.37 = (bf16[1536,1024]{1,0:T(8,128)(2,1)}, bf16[1536,1024]{1,0:T(8,128)(2,1)}) custom-call(bf16[512,1024]{1,0:T(8,128)(2,1)} %bitcast.6, bf16[512,1024]{1,0:T(8,128)(2,1)} %broadcast_in_dim.52.zeros_ref), custom_call_target="tpu_custom_call" | custom-call | tf_op jit(solution)/shard_map/pallas_call | solution.py:136
  122.0 1.6 %broadcast_compare_fusion = pred[1536,1536]{1,0:T(32,128)(4,1)S(1)} fusion(s32[1536]{0:T(1024)S(1)} %get-tuple-element.10, s32[1536]{0:T(1024)S(1)} %get-tuple-element.9), kind=kLoop, calls=%fused_computation.3 | loop fusion | flops 2359296 | bytes 2371584 | tf_op jit(solution)/shard_map/eq | solution.py:179
  123.7 8.5 %select_reduce_fusion.1 = (f32[1536]{0:T(1024)S(1)}, f32[1536,1536]{1,0:T(8,128)S(1)}) fusion(s32[1536]{0:T(1024)S(1)} %get-tuple-element.10, s32[1536]{0:T(1024)S(1)} %get-tuple-element.9, bf16[1536,1024]{1,0:T(8,128)(2,1)} %get-tuple-element.7, bf16[1536,1024]{1,0:T(8,128)(2,1)} %get-tuple-element.8), kind=kOutput, calls=%fused_computation.2 | convolution fusion | flops 4841273856 | bytes 15747072 | tf_op jit(solution)/shard_map/dot_general | solution.py:181
  132.1 0.0 copy-start
  132.1 0.6 select_reduce_fusion.3
  132.8 0.9 select_reduce_fusion.2
  133.7 2.0 %copy-done = f32[1536,1536]{1,0:T(8,128)} copy-done((f32[1536,1536]{1,0:T(8,128)}, f32[1536,1536]{1,0:T(8,128)S(1)}, u32[]{:S(2)}) %copy-start) | copy-done | bytes 9437208
  135.8 0.0 copy-start.1
  135.8 2.3 %select_reduce_fusion = f32[1536]{0:T(1024)S(1)} fusion(f32[1536,1536]{1,0:T(8,128)S(1)} %get-tuple-element.12, f32[1536]{0:T(1024)S(1)} %is-finite_select_fusion, s32[1536]{0:T(1024)S(1)} %get-tuple-element.10, s32[1536]{0:T(1024)S(1)} %get-tuple-element.9), kind=kLoop, calls=%fused_computation.1 | loop fusion | flops 9435648 | bytes 9461760 | tf_op jit(solution)/shard_map/reduce_sum | solution.py:157
  138.1 0.0 collective-permute-done
  138.1 0.0 collective-permute-done.1
  138.1 0.0 copy-done.1
  138.2 6.9 %fusion.8 = bf16[1,512,1024]{2,1,0:T(8,128)(2,1)} fusion(bf16[1536,1024]{1,0:T(8,128)(2,1)} %get-tuple-element.8, f32[1536,1536]{1,0:T(8,128)} %copy-done, pred[1536,1536]{1,0:T(32,128)(4,1)S(1)} %broadcast_compare_fusion, s32[1536]{0:T(1024)S(1)} %pad_add_fusion, s32[1536]{0:T(1024)S(1)} %iota_add_fusion, f32[1536]{0:T(1024)S(1)} %log_add_fusion, ...), kind=kOutput, calls=%fused_computation.16 | convolution fusion | flops 1619525632 | bytes 8157185 | tf_op jit(solution)/shard_map/dot_general | solution.py:198
  (9 shorter events, 0.1 us)
Async XLA Ops:
  0.0 138.1 %collective-permute-start = (s32[512]{0:T(512)}, s32[512]{0:T(512)S(1)}, u32[]{:S(2)}, u32[]{:S(2)}) collective-permute-start(s32[512]{0:T(512)} %param.5), channel_id=1, source_target_pairs={{0,1},{1,2},{2,3},{3,4},{4,5},{5,6},{6,7},{7,8},{8,9},{9,10},{10,1... | collective-permute-start | bytes 6152 | tf_op jit(solution)/shard_map/ppermute | solution.py:24
  1.7 136.4 %collective-permute-start.1 = (s32[512]{0:T(512)}, s32[512]{0:T(512)S(1)}, u32[]{:S(2)}, u32[]{:S(2)}) collective-permute-start(s32[512]{0:T(512)} %param.5), channel_id=1, source_target_pairs={{1,0},{2,1},{3,2},{4,3},{5,4},{6,5},{7,6},{8,7},{9,8},{10,9},{11,1... | collective-permute-start | bytes 6152 | tf_op jit(solution)/shard_map/ppermute | solution.py:25
  132.1 3.6 %copy-start = (f32[1536,1536]{1,0:T(8,128)}, f32[1536,1536]{1,0:T(8,128)S(1)}, u32[]{:S(2)}) copy-start(f32[1536,1536]{1,0:T(8,128)S(1)} %get-tuple-element.12) | copy-start | bytes 28311556
  135.8 2.4 %copy-start.1 = (s32[512]{0:T(512)S(1)}, s32[512]{0:T(512)}, u32[]{:S(2)}) copy-start(s32[512]{0:T(512)} %param.5) | copy-start | bytes 6148

commit v3 on v2

--- a/solution.py
+++ b/solution.py
@@ -30,7 +30,7 @@
 CHUNKS = 4
 
 
-def exchange_kernel(groups, own_ref, zeros_ref, own_win, partner_win, local_sem,
+def exchange_kernel(groups, own_ref, own_out, partner_out, own_win, partner_win, local_sem,
                     sec_send, sec_recv, fwd_send, fwd_recv, halo_send, halo_recv):
     rows = own_ref.shape[0]
     piece = rows // CHUNKS
@@ -45,6 +45,16 @@
     left_id = (sec, (me - 1) // groups, (me - 1) % groups)
     right_id = (sec, (me + 1) // groups, (me + 1) % groups)
 
+    centre = pltpu.make_async_copy(own_ref, own_win.at[pl.ds(rows, rows)], local_sem.at[0])
+    centre.start()
+
+    for d, arrived in ((0, has_right), (1, has_left)):
+        @pl.when(jnp.logical_not(arrived))
+        def _():
+            place = pl.ds((1 - d) * 2 * rows, rows)
+            own_win[place, :] = jnp.zeros((rows, own_win.shape[1]), own_win.dtype)
+            partner_win[place, :] = jnp.zeros((rows, own_win.shape[1]), own_win.dtype)
+
     barrier = pltpu.get_barrier_semaphore()
     pl.semaphore_signal(barrier, 1, device_id=partner_id, device_id_type=MESH_ID)
 
@@ -88,9 +98,6 @@
         def _():
             halo_copy(d).start()
 
-    centre = pltpu.make_async_copy(own_ref, own_win.at[pl.ds(rows, rows)], local_sem.at[0])
-    centre.start()
-
     for c in range(CHUNKS):
         sec_copy(c).wait_recv()
         for d, present in sides:
@@ -116,17 +123,12 @@
     for c in range(CHUNKS):
         sec_copy(c).wait_send()
     centre.wait()
-
-    for d, arrived in ((0, has_right), (1, has_left)):
-        @pl.when(jnp.logical_not(arrived))
-        def _():
-            place = pl.ds((1 - d) * 2 * rows, rows)
-            first = pltpu.make_async_copy(zeros_ref, own_win.at[place], local_sem.at[1])
-            second = pltpu.make_async_copy(zeros_ref, partner_win.at[place], local_sem.at[2])
-            first.start()
-            second.start()
-            first.wait()
-            second.wait()
+    first = pltpu.make_async_copy(own_win, own_out, local_sem.at[1])
+    second = pltpu.make_async_copy(partner_win, partner_out, local_sem.at[2])
+    first.start()
+    second.start()
+    first.wait()
+    second.wait()
 
 
 def exchange(own, groups):
@@ -136,9 +138,11 @@
     return pl.pallas_call(
         functools.partial(exchange_kernel, groups),
         out_shape=(window, window),
-        in_specs=[anywhere, anywhere],
+        in_specs=[anywhere],
         out_specs=(anywhere, anywhere),
         scratch_shapes=[
+            pltpu.VMEM((3 * rows, features), own.dtype),
+            pltpu.VMEM((3 * rows, features), own.dtype),
             pltpu.SemaphoreType.DMA((3,)),
             pltpu.SemaphoreType.DMA((CHUNKS,)),
             pltpu.SemaphoreType.DMA((CHUNKS,)),
@@ -147,8 +151,10 @@
             pltpu.SemaphoreType.DMA((2,)),
             pltpu.SemaphoreType.DMA((2,)),
         ],
-        compiler_params=pltpu.CompilerParams(collective_id=0, has_side_effects=True),
-    )(own, jnp.zeros_like(own))
+        compiler_params=pltpu.CompilerParams(
+            collective_id=0, has_side_effects=True, vmem_limit_bytes=32 * 1024 * 1024
+        ),
+    )(own)
 
 
 def masked_lse(scores, allowed, axis):

time: 145 us -> 89.3 us (0.62)
  the two profiles are of different devices: /device:TPU:4 before, /device:TPU:251 now
where the time goes in v3:
time: 89.3 us; the launch traced here: 89.1 us
  Pallas kernels  60.9 us (68%)
  matrix products  11.7 us (13%)
  starting transfers between devices  6.86 us (8%)
  other arithmetic  5.49 us (6%)
  local copies, waits for them, and re-layouts  4.12 us (5%)
    pallas_call x1, Pallas kernels, exchange(): pl.pallas_call(functools.partial(exchange_kernel, groups), out_shape=(win...  60.9 us
    dot_general x1, matrix products, local(): jnp.dot(weights.astype(jnp.bfloat16), partner_win, preferred_element_type...  6.02 us
    dot_general x1, matrix products, local(): lax.dot_general(own_win, partner_win, (((1,), (1,)), ((), ())), preferred...  5.63 us
    ppermute x1, starting transfers between devices, neighbours(): from_left = lax.ppermute(value, axis, forward)  4.94 us
    unnamed x8, local copies, waits for them, and re-layouts  3.28 us
    reduce_sum x2, other arithmetic, masked_lse(): jnp.sum(jnp.where(allowed, jnp.exp(scores - top), 0.0), axis=axis, keepdi...  3.17 us
    ppermute x1, starting transfers between devices, neighbours(): from_right = lax.ppermute(value, axis, backward)  1.92 us
  transfers between devices with their start and end apart: 2, of which 0 were waited for; matrix products, arithmetic and copies ran while one was open for 13% of the time, Pallas kernels for 68%

profile of v3, /device:TPU:251, one launch (start us, length us, event | category | flops | bytes accessed | tf_op | source)
XLA Modules:
  0.0 89.1 jit_solution(10573954967285141889)
XLA Ops:
  0.0 4.9 %collective-permute-start = (s32[512]{0:T(512)}, s32[512]{0:T(512)S(1)}, u32[]{:S(2)}, u32[]{:S(2)}) collective-permute-start(s32[512]{0:T(512)} %param.5), channel_id=1, source_target_pairs={{0,1},{1,2},{2,3},{3,4},{4,5},{5,6},{6,7},{7,8},{8,9},{9,10},{10,1... | collective-permute-start | bytes 6152 | tf_op jit(solution)/shard_map/ppermute | solution.py:24
  4.9 1.9 %collective-permute-start.1 = (s32[512]{0:T(512)}, s32[512]{0:T(512)S(1)}, u32[]{:S(2)}, u32[]{:S(2)}) collective-permute-start(s32[512]{0:T(512)} %param.5), channel_id=1, source_target_pairs={{1,0},{2,1},{3,2},{4,3},{5,4},{6,5},{7,6},{8,7},{9,8},{10,9},{11,1... | collective-permute-start | bytes 6152 | tf_op jit(solution)/shard_map/ppermute | solution.py:25
  6.9 0.8 pad_dynamic-slice_fusion
  7.7 0.1 broadcast_in_dim.46
  7.7 0.0 copy-start
  7.7 1.2 %copy-done = bf16[1,512,1024]{2,1,0:T(8,128)(2,1)S(1)} copy-done((bf16[1,512,1024]{2,1,0:T(8,128)(2,1)S(1)}, bf16[1,512,1024]{2,1,0:T(8,128)(2,1)}, u32[]{:S(2)}) %copy-start) | copy-done | bytes 1048600
  9.0 60.9 %shard_map.37 = (bf16[1536,1024]{1,0:T(8,128)(2,1)S(1)}, bf16[1536,1024]{1,0:T(8,128)(2,1)S(1)}) custom-call(bf16[512,1024]{1,0:T(8,128)(2,1)S(1)} %bitcast.6), custom_call_target="tpu_custom_call" | custom-call | tf_op jit(solution)/shard_map/pallas_call | solution.py:138
  69.8 1.6 %broadcast_compare_fusion = pred[1536,1536]{1,0:T(32,128)(4,1)S(1)} fusion(s32[1536]{0:T(1024)S(1)} %get-tuple-element.10, s32[1536]{0:T(1024)S(1)} %get-tuple-element.9), kind=kLoop, calls=%fused_computation.3 | loop fusion | flops 2359296 | bytes 2371584 | tf_op jit(solution)/shard_map/eq | solution.py:185
  71.5 0.0 copy-start.2
  71.5 5.6 %select_reduce_fusion.1 = (f32[1536]{0:T(1024)S(1)}, f32[1536,1536]{1,0:T(8,128)S(1)}) fusion(s32[1536]{0:T(1024)S(1)} %get-tuple-element.10, s32[1536]{0:T(1024)S(1)} %get-tuple-element.9, bf16[1536,1024]{1,0:T(8,128)(2,1)S(1)} %get-tuple-element.7, bf16[1536,1024]{1,0:T(8,128)(2,1)S(1)} %get-tuple-element.8), kind=kOutput, calls=%fused_computation.2 | convolution fusion | flops 4841273856 | bytes 15747072 | tf_op jit(solution)/shard_map/dot_general | solution.py:187
  77.1 0.0 copy-start.1
  77.1 0.6 select_reduce_fusion.3
  77.8 0.0 copy-done.2
  77.8 0.9 %select_reduce_fusion.2 = f32[512]{0:T(512)S(1)} fusion(f32[1536,1536]{1,0:T(8,128)S(1)} %get-tuple-element.12, pred[1536,1536]{1,0:T(32,128)(4,1)S(1)} %broadcast_compare_fusion, f32[512]{0:T(512)S(1)} %is-finite_select_fusion.1), kind=kLoop, calls=%fused_computation.5 | loop fusion | flops 2358784 | bytes 3936256 | tf_op jit(solution)/shard_map/reduce_sum | solution.py:163
  78.7 2.0 %copy-done.1 = f32[1536,1536]{1,0:T(8,128)} copy-done((f32[1536,1536]{1,0:T(8,128)}, f32[1536,1536]{1,0:T(8,128)S(1)}, u32[]{:S(2)}) %copy-start.1) | copy-done | bytes 9437208
  80.7 0.0 copy-start.3
  80.7 2.3 %select_reduce_fusion = f32[1536]{0:T(1024)S(1)} fusion(f32[1536,1536]{1,0:T(8,128)S(1)} %get-tuple-element.12, f32[1536]{0:T(1024)S(1)} %is-finite_select_fusion, s32[1536]{0:T(1024)S(1)} %get-tuple-element.10, s32[1536]{0:T(1024)S(1)} %get-tuple-element.9), kind=kLoop, calls=%fused_computation.1 | loop fusion | flops 9435648 | bytes 9461760 | tf_op jit(solution)/shard_map/reduce_sum | solution.py:163
  83.1 0.0 collective-permute-done
  83.1 0.0 collective-permute-done.1
  83.1 0.0 copy-done.3
  83.1 6.0 %fusion.8 = bf16[1,512,1024]{2,1,0:T(8,128)(2,1)} fusion(bf16[1536,1024]{1,0:T(8,128)(2,1)S(1)} %get-tuple-element.8, f32[1536,1536]{1,0:T(8,128)} %copy-done.1, pred[1536,1536]{1,0:T(32,128)(4,1)} %copy-done.2, s32[1536]{0:T(1024)S(1)} %pad_add_fusion, s32[1536]{0:T(1024)S(1)} %iota_add_fusion, f32[1536]{0:T(1024)S(1)} %log_add_fusion, ...), kind=kOutput, calls=%fused_computation.16 | convolution fusion | flops 1619525632 | bytes 8151041 | tf_op jit(solution)/shard_map/dot_general | solution.py:204
  (9 shorter events, 0.1 us)
Async XLA Ops:
  0.0 83.1 %collective-permute-start = (s32[512]{0:T(512)}, s32[512]{0:T(512)S(1)}, u32[]{:S(2)}, u32[]{:S(2)}) collective-permute-start(s32[512]{0:T(512)} %param.5), channel_id=1, source_target_pairs={{0,1},{1,2},{2,3},{3,4},{4,5},{5,6},{6,7},{7,8},{8,9},{9,10},{10,1... | collective-permute-start | bytes 6152 | tf_op jit(solution)/shard_map/ppermute | solution.py:24
  4.9 78.1 %collective-permute-start.1 = (s32[512]{0:T(512)}, s32[512]{0:T(512)S(1)}, u32[]{:S(2)}, u32[]{:S(2)}) collective-permute-start(s32[512]{0:T(512)} %param.5), channel_id=1, source_target_pairs={{1,0},{2,1},{3,2},{4,3},{5,4},{6,5},{7,6},{8,7},{9,8},{10,9},{11,1... | collective-permute-start | bytes 6152 | tf_op jit(solution)/shard_map/ppermute | solution.py:25
  7.7 1.2 %copy-start = (bf16[1,512,1024]{2,1,0:T(8,128)(2,1)S(1)}, bf16[1,512,1024]{2,1,0:T(8,128)(2,1)}, u32[]{:S(2)}) copy-start(bf16[1,512,1024]{2,1,0:T(8,128)(2,1)} %param.3) | copy-start | bytes 3145732
  71.5 6.3 %copy-start.2 = (pred[1536,1536]{1,0:T(32,128)(4,1)}, pred[1536,1536]{1,0:T(32,128)(4,1)S(1)}, u32[]{:S(2)}) copy-start(pred[1536,1536]{1,0:T(32,128)(4,1)S(1)} %broadcast_compare_fusion) | copy-start | bytes 7077892
  77.1 3.6 %copy-start.1 = (f32[1536,1536]{1,0:T(8,128)}, f32[1536,1536]{1,0:T(8,128)S(1)}, u32[]{:S(2)}) copy-start(f32[1536,1536]{1,0:T(8,128)S(1)} %get-tuple-element.12) | copy-start | bytes 28311556
  80.7 2.4 %copy-start.3 = (s32[512]{0:T(512)S(1)}, s32[512]{0:T(512)}, u32[]{:S(2)}) copy-start(s32[512]{0:T(512)} %param.5) | copy-start | bytes 6148

commit v4 on v3

--- a/solution.py
+++ b/solution.py
@@ -27,13 +27,16 @@
 
 
 MESH_ID = pl.DeviceIdType.MESH
-CHUNKS = 4
-
-
-def exchange_kernel(groups, own_ref, own_out, partner_out, own_win, partner_win, local_sem,
-                    sec_send, sec_recv, fwd_send, fwd_recv, halo_send, halo_recv):
+PIECES = 2
+Y_CHIPS = 8
+
+
+def exchange_kernel(groups, own_ref, own_out, partner_out, own_win, partner_win, relay,
+                    local_sem, hop_send, hop_recv, last_send, last_recv, fwd_send, fwd_recv,
+                    halo_send, halo_recv):
     rows = own_ref.shape[0]
-    piece = rows // CHUNKS
+    half = rows // 2
+    piece = half // PIECES
     sec = lax.axis_index("sec")
     wide = lax.axis_index("wide")
     grp = lax.axis_index("grp")
@@ -41,9 +44,11 @@
     me = wide * groups + grp
     has_left = me > 0
     has_right = me < count - 1
-    partner_id = (1 - sec, wide, grp)
     left_id = (sec, (me - 1) // groups, (me - 1) % groups)
     right_id = (sec, (me + 1) // groups, (me + 1) % groups)
+    ring = Y_CHIPS
+    flipped = jnp.where((wide // ring) % 2 == 0, wide + ring, wide - ring)
+    relay_id = ((sec, flipped, grp), (1 - sec, flipped, grp))
 
     centre = pltpu.make_async_copy(own_ref, own_win.at[pl.ds(rows, rows)], local_sem.at[0])
     centre.start()
@@ -56,7 +61,8 @@
             partner_win[place, :] = jnp.zeros((rows, own_win.shape[1]), own_win.dtype)
 
     barrier = pltpu.get_barrier_semaphore()
-    pl.semaphore_signal(barrier, 1, device_id=partner_id, device_id_type=MESH_ID)
+    for k in range(2):
+        pl.semaphore_signal(barrier, 1, device_id=relay_id[k], device_id_type=MESH_ID)
 
     @pl.when(has_left)
     def _():
@@ -66,15 +72,22 @@
     def _():
         pl.semaphore_signal(barrier, 1, device_id=right_id, device_id_type=MESH_ID)
 
-    peers = 1 + has_left.astype(jnp.int32) + has_right.astype(jnp.int32)
+    peers = 2 + has_left.astype(jnp.int32) + has_right.astype(jnp.int32)
     pl.semaphore_wait(barrier, peers)
 
-    def sec_copy(c):
-        return pltpu.make_async_remote_copy(
-            src_ref=own_ref.at[pl.ds(c * piece, piece)],
-            dst_ref=partner_win.at[pl.ds(rows + c * piece, piece)],
-            send_sem=sec_send.at[c], recv_sem=sec_recv.at[c],
-            device_id=partner_id, device_id_type=MESH_ID)
+    def hop(k, p):
+        return pltpu.make_async_remote_copy(
+            src_ref=own_ref.at[pl.ds(k * half + p * piece, piece)],
+            dst_ref=relay.at[k, pl.ds(p * piece, piece)],
+            send_sem=hop_send.at[k, p], recv_sem=hop_recv.at[k, p],
+            device_id=relay_id[k], device_id_type=MESH_ID)
+
+    def last(k, p):
+        return pltpu.make_async_remote_copy(
+            src_ref=relay.at[k, pl.ds(p * piece, piece)],
+            dst_ref=partner_win.at[pl.ds(rows + k * half + p * piece, piece)],
+            send_sem=last_send.at[k, p], recv_sem=last_recv.at[k, p],
+            device_id=relay_id[1 - k], device_id_type=MESH_ID)
 
     def halo_copy(d):
         return pltpu.make_async_remote_copy(
@@ -83,45 +96,54 @@
             send_sem=halo_send.at[d], recv_sem=halo_recv.at[d],
             device_id=left_id if d == 0 else right_id, device_id_type=MESH_ID)
 
-    def fwd_copy(d, c):
-        return pltpu.make_async_remote_copy(
-            src_ref=partner_win.at[pl.ds(rows + c * piece, piece)],
-            dst_ref=partner_win.at[pl.ds((1 - d) * 2 * rows + c * piece, piece)],
-            send_sem=fwd_send.at[d, c], recv_sem=fwd_recv.at[d, c],
+    def fwd_copy(d, q):
+        return pltpu.make_async_remote_copy(
+            src_ref=partner_win.at[pl.ds(rows + q * piece, piece)],
+            dst_ref=partner_win.at[pl.ds((1 - d) * 2 * rows + q * piece, piece)],
+            send_sem=fwd_send.at[d, q], recv_sem=fwd_recv.at[d, q],
             device_id=left_id if d == 0 else right_id, device_id_type=MESH_ID)
 
-    for c in range(CHUNKS):
-        sec_copy(c).start()
+    for p in range(PIECES):
+        for k in range(2):
+            hop(k, p).start()
     sides = ((0, has_left), (1, has_right))
     for d, present in sides:
         @pl.when(present)
         def _():
             halo_copy(d).start()
 
-    for c in range(CHUNKS):
-        sec_copy(c).wait_recv()
-        for d, present in sides:
-            @pl.when(present)
-            def _():
-                fwd_copy(d, c).start()
+    for p in range(PIECES):
+        for k in range(2):
+            hop(k, p).wait_recv()
+            last(k, p).start()
+    for p in range(PIECES):
+        for k in range(2):
+            last(k, p).wait_recv()
+            q = k * PIECES + p
+            for d, present in sides:
+                @pl.when(present)
+                def _():
+                    fwd_copy(d, q).start()
 
     for d, present in sides:
         @pl.when(present)
         def _():
             halo_copy(d).wait_send()
-            for c in range(CHUNKS):
-                fwd_copy(d, c).wait_send()
+            for q in range(2 * PIECES):
+                fwd_copy(d, q).wait_send()
 
         arrived = has_right if d == 0 else has_left
 
         @pl.when(arrived)
         def _():
             halo_copy(d).wait_recv()
-            for c in range(CHUNKS):
-                fwd_copy(d, c).wait_recv()
-
-    for c in range(CHUNKS):
-        sec_copy(c).wait_send()
+            for q in range(2 * PIECES):
+                fwd_copy(d, q).wait_recv()
+
+    for p in range(PIECES):
+        for k in range(2):
+            hop(k, p).wait_send()
+            last(k, p).wait_send()
     centre.wait()
     first = pltpu.make_async_copy(own_win, own_out, local_sem.at[1])
     second = pltpu.make_async_copy(partner_win, partner_out, local_sem.at[2])
@@ -143,11 +165,14 @@
         scratch_shapes=[
             pltpu.VMEM((3 * rows, features), own.dtype),
             pltpu.VMEM((3 * rows, features), own.dtype),
+            pltpu.VMEM((2, rows // 2, features), own.dtype),
             pltpu.SemaphoreType.DMA((3,)),
-            pltpu.SemaphoreType.DMA((CHUNKS,)),
-            pltpu.SemaphoreType.DMA((CHUNKS,)),
-            pltpu.SemaphoreType.DMA((2, CHUNKS)),
-            pltpu.SemaphoreType.DMA((2, CHUNKS)),
+            pltpu.SemaphoreType.DMA((2, PIECES)),
+            pltpu.SemaphoreType.DMA((2, PIECES)),
+            pltpu.SemaphoreType.DMA((2, PIECES)),
+            pltpu.SemaphoreType.DMA((2, PIECES)),
+            pltpu.SemaphoreType.DMA((2, 2 * PIECES)),
+            pltpu.SemaphoreType.DMA((2, 2 * PIECES)),
             pltpu.SemaphoreType.DMA((2,)),
             pltpu.SemaphoreType.DMA((2,)),
         ],

time: 89.3 us -> 85.8 us (0.961)
  Pallas kernels: 60.9 us -> 57.3 us
    pallas_call x1, Pallas kernels: 60.9 us -> 57.3 us  [exchange(): pl.pallas_call(functools.partial(exchange_kernel, groups), out_shape=(win...]
  transfers between devices with their start and end apart: 2 -> 2, of which waited for: 0 -> 0; matrix products, arithmetic and copies ran while one was open for 13% -> 14% of each run, Pallas kernels for 68% -> 67%
where the time goes in v4:
time: 85.8 us; the launch traced here: 85.6 us
  Pallas kernels  57.3 us (67%)
  matrix products  11.6 us (14%)
  starting transfers between devices  6.86 us (8%)
  other arithmetic  5.49 us (6%)
  local copies, waits for them, and re-layouts  4.12 us (5%)
    pallas_call x1, Pallas kernels, exchange(): pl.pallas_call(functools.partial(exchange_kernel, groups), out_shape=(win...  57.3 us
    dot_general x1, matrix products, local(): jnp.dot(weights.astype(jnp.bfloat16), partner_win, preferred_element_type...  6.02 us
    dot_general x1, matrix products, local(): lax.dot_general(own_win, partner_win, (((1,), (1,)), ((), ())), preferred...  5.63 us
    ppermute x1, starting transfers between devices, neighbours(): from_left = lax.ppermute(value, axis, forward)  4.94 us
    unnamed x8, local copies, waits for them, and re-layouts  3.28 us
    reduce_sum x2, other arithmetic, masked_lse(): jnp.sum(jnp.where(allowed, jnp.exp(scores - top), 0.0), axis=axis, keepdi...  3.17 us
    ppermute x1, starting transfers between devices, neighbours(): from_right = lax.ppermute(value, axis, backward)  1.92 us
  transfers between devices with their start and end apart: 2, of which 0 were waited for; matrix products, arithmetic and copies ran while one was open for 14% of the time, Pallas kernels for 67%

profile of v4, /device:TPU:251, one launch (start us, length us, event | category | flops | bytes accessed | tf_op | source)
XLA Modules:
  0.0 85.6 jit_solution(11237788766637820442)
XLA Ops:
  0.0 4.9 %collective-permute-start = (s32[512]{0:T(512)}, s32[512]{0:T(512)S(1)}, u32[]{:S(2)}, u32[]{:S(2)}) collective-permute-start(s32[512]{0:T(512)} %param.5), channel_id=1, source_target_pairs={{0,1},{1,2},{2,3},{3,4},{4,5},{5,6},{6,7},{7,8},{8,9},{9,10},{10,1... | collective-permute-start | bytes 6152 | tf_op jit(solution)/shard_map/ppermute | solution.py:24
  4.9 1.9 %collective-permute-start.1 = (s32[512]{0:T(512)}, s32[512]{0:T(512)S(1)}, u32[]{:S(2)}, u32[]{:S(2)}) collective-permute-start(s32[512]{0:T(512)} %param.5), channel_id=1, source_target_pairs={{1,0},{2,1},{3,2},{4,3},{5,4},{6,5},{7,6},{8,7},{9,8},{10,9},{11,1... | collective-permute-start | bytes 6152 | tf_op jit(solution)/shard_map/ppermute | solution.py:25
  6.9 0.8 pad_dynamic-slice_fusion
  7.7 0.1 broadcast_in_dim.46
  7.7 0.0 copy-start
  7.7 1.2 %copy-done = bf16[1,512,1024]{2,1,0:T(8,128)(2,1)S(1)} copy-done((bf16[1,512,1024]{2,1,0:T(8,128)(2,1)S(1)}, bf16[1,512,1024]{2,1,0:T(8,128)(2,1)}, u32[]{:S(2)}) %copy-start) | copy-done | bytes 1048600
  9.0 57.3 %shard_map.37 = (bf16[1536,1024]{1,0:T(8,128)(2,1)S(1)}, bf16[1536,1024]{1,0:T(8,128)(2,1)S(1)}) custom-call(bf16[512,1024]{1,0:T(8,128)(2,1)S(1)} %bitcast.6), custom_call_target="tpu_custom_call" | custom-call | tf_op jit(solution)/shard_map/pallas_call | solution.py:160
  66.3 1.6 %broadcast_compare_fusion = pred[1536,1536]{1,0:T(32,128)(4,1)S(1)} fusion(s32[1536]{0:T(1024)S(1)} %get-tuple-element.10, s32[1536]{0:T(1024)S(1)} %get-tuple-element.9), kind=kLoop, calls=%fused_computation.3 | loop fusion | flops 2359296 | bytes 2371584 | tf_op jit(solution)/shard_map/eq | solution.py:210
  67.9 0.0 copy-start.2
  67.9 5.6 %select_reduce_fusion.1 = (f32[1536]{0:T(1024)S(1)}, f32[1536,1536]{1,0:T(8,128)S(1)}) fusion(s32[1536]{0:T(1024)S(1)} %get-tuple-element.10, s32[1536]{0:T(1024)S(1)} %get-tuple-element.9, bf16[1536,1024]{1,0:T(8,128)(2,1)S(1)} %get-tuple-element.7, bf16[1536,1024]{1,0:T(8,128)(2,1)S(1)} %get-tuple-element.8), kind=kOutput, calls=%fused_computation.2 | convolution fusion | flops 4841273856 | bytes 15747072 | tf_op jit(solution)/shard_map/dot_general | solution.py:212
  73.6 0.0 copy-start.1
  73.6 0.6 select_reduce_fusion.3
  74.2 0.0 copy-done.2
  74.2 0.9 %select_reduce_fusion.2 = f32[512]{0:T(512)S(1)} fusion(f32[1536,1536]{1,0:T(8,128)S(1)} %get-tuple-element.12, pred[1536,1536]{1,0:T(32,128)(4,1)S(1)} %broadcast_compare_fusion, f32[512]{0:T(512)S(1)} %is-finite_select_fusion.1), kind=kLoop, calls=%fused_computation.5 | loop fusion | flops 2358784 | bytes 3936256 | tf_op jit(solution)/shard_map/reduce_sum | solution.py:188
  75.1 2.0 %copy-done.1 = f32[1536,1536]{1,0:T(8,128)} copy-done((f32[1536,1536]{1,0:T(8,128)}, f32[1536,1536]{1,0:T(8,128)S(1)}, u32[]{:S(2)}) %copy-start.1) | copy-done | bytes 9437208
  77.2 0.0 copy-start.3
  77.2 2.3 %select_reduce_fusion = f32[1536]{0:T(1024)S(1)} fusion(f32[1536,1536]{1,0:T(8,128)S(1)} %get-tuple-element.12, f32[1536]{0:T(1024)S(1)} %is-finite_select_fusion, s32[1536]{0:T(1024)S(1)} %get-tuple-element.10, s32[1536]{0:T(1024)S(1)} %get-tuple-element.9), kind=kLoop, calls=%fused_computation.1 | loop fusion | flops 9435648 | bytes 9461760 | tf_op jit(solution)/shard_map/reduce_sum | solution.py:188
  79.5 0.0 collective-permute-done
  79.5 0.0 collective-permute-done.1
  79.5 0.0 copy-done.3
  79.6 6.0 %fusion.8 = bf16[1,512,1024]{2,1,0:T(8,128)(2,1)} fusion(bf16[1536,1024]{1,0:T(8,128)(2,1)S(1)} %get-tuple-element.8, f32[1536,1536]{1,0:T(8,128)} %copy-done.1, pred[1536,1536]{1,0:T(32,128)(4,1)} %copy-done.2, s32[1536]{0:T(1024)S(1)} %pad_add_fusion, s32[1536]{0:T(1024)S(1)} %iota_add_fusion, f32[1536]{0:T(1024)S(1)} %log_add_fusion, ...), kind=kOutput, calls=%fused_computation.16 | convolution fusion | flops 1619525632 | bytes 8151041 | tf_op jit(solution)/shard_map/dot_general | solution.py:229
  (9 shorter events, 0.1 us)
Async XLA Ops:
  0.0 79.5 %collective-permute-start = (s32[512]{0:T(512)}, s32[512]{0:T(512)S(1)}, u32[]{:S(2)}, u32[]{:S(2)}) collective-permute-start(s32[512]{0:T(512)} %param.5), channel_id=1, source_target_pairs={{0,1},{1,2},{2,3},{3,4},{4,5},{5,6},{6,7},{7,8},{8,9},{9,10},{10,1... | collective-permute-start | bytes 6152 | tf_op jit(solution)/shard_map/ppermute | solution.py:24
  4.9 74.6 %collective-permute-start.1 = (s32[512]{0:T(512)}, s32[512]{0:T(512)S(1)}, u32[]{:S(2)}, u32[]{:S(2)}) collective-permute-start(s32[512]{0:T(512)} %param.5), channel_id=1, source_target_pairs={{1,0},{2,1},{3,2},{4,3},{5,4},{6,5},{7,6},{8,7},{9,8},{10,9},{11,1... | collective-permute-start | bytes 6152 | tf_op jit(solution)/shard_map/ppermute | solution.py:25
  7.7 1.2 %copy-start = (bf16[1,512,1024]{2,1,0:T(8,128)(2,1)S(1)}, bf16[1,512,1024]{2,1,0:T(8,128)(2,1)}, u32[]{:S(2)}) copy-start(bf16[1,512,1024]{2,1,0:T(8,128)(2,1)} %param.3) | copy-start | bytes 3145732
  67.9 6.3 %copy-start.2 = (pred[1536,1536]{1,0:T(32,128)(4,1)}, pred[1536,1536]{1,0:T(32,128)(4,1)S(1)}, u32[]{:S(2)}) copy-start(pred[1536,1536]{1,0:T(32,128)(4,1)S(1)} %broadcast_compare_fusion) | copy-start | bytes 7077892
  73.6 3.6 %copy-start.1 = (f32[1536,1536]{1,0:T(8,128)}, f32[1536,1536]{1,0:T(8,128)S(1)}, u32[]{:S(2)}) copy-start(f32[1536,1536]{1,0:T(8,128)S(1)} %get-tuple-element.12) | copy-start | bytes 28311556
  77.2 2.4 %copy-start.3 = (s32[512]{0:T(512)S(1)}, s32[512]{0:T(512)}, u32[]{:S(2)}) copy-start(s32[512]{0:T(512)} %param.5) | copy-start | bytes 6148

commit v5 on v4

--- a/solution.py
+++ b/solution.py
@@ -31,9 +31,9 @@
 Y_CHIPS = 8
 
 
-def exchange_kernel(groups, own_ref, own_out, partner_out, own_win, partner_win, relay,
-                    local_sem, hop_send, hop_recv, last_send, last_recv, fwd_send, fwd_recv,
-                    halo_send, halo_recv):
+def exchange_kernel(groups, own_ref, pos_ref, own_out, partner_out, pos_out, own_win,
+                    partner_win, pos_win, relay, local_sem, hop_send, hop_recv, last_send,
+                    last_recv, fwd_send, fwd_recv, halo_send, halo_recv):
     rows = own_ref.shape[0]
     half = rows // 2
     piece = half // PIECES
@@ -52,6 +52,9 @@
 
     centre = pltpu.make_async_copy(own_ref, own_win.at[pl.ds(rows, rows)], local_sem.at[0])
     centre.start()
+    lines = pos_ref.shape[0]
+    pos_centre = pltpu.make_async_copy(pos_ref, pos_win.at[pl.ds(lines, lines)], local_sem.at[3])
+    pos_centre.start()
 
     for d, arrived in ((0, has_right), (1, has_left)):
         @pl.when(jnp.logical_not(arrived))
@@ -59,6 +62,7 @@
             place = pl.ds((1 - d) * 2 * rows, rows)
             own_win[place, :] = jnp.zeros((rows, own_win.shape[1]), own_win.dtype)
             partner_win[place, :] = jnp.zeros((rows, own_win.shape[1]), own_win.dtype)
+            pos_win[pl.ds((1 - d) * 2 * lines, lines), :] = jnp.zeros(pos_ref.shape, jnp.int32)
 
     barrier = pltpu.get_barrier_semaphore()
     for k in range(2):
@@ -96,6 +100,13 @@
             send_sem=halo_send.at[d], recv_sem=halo_recv.at[d],
             device_id=left_id if d == 0 else right_id, device_id_type=MESH_ID)
 
+    def pos_copy(d):
+        return pltpu.make_async_remote_copy(
+            src_ref=pos_ref,
+            dst_ref=pos_win.at[pl.ds((1 - d) * 2 * lines, lines)],
+            send_sem=halo_send.at[2 + d], recv_sem=halo_recv.at[2 + d],
+            device_id=left_id if d == 0 else right_id, device_id_type=MESH_ID)
+
     def fwd_copy(d, q):
         return pltpu.make_async_remote_copy(
             src_ref=partner_win.at[pl.ds(rows + q * piece, piece)],
@@ -110,6 +121,7 @@
     for d, present in sides:
         @pl.when(present)
         def _():
+            pos_copy(d).start()
             halo_copy(d).start()
 
     for p in range(PIECES):
@@ -128,6 +140,7 @@
     for d, present in sides:
         @pl.when(present)
         def _():
+            pos_copy(d).wait_send()
             halo_copy(d).wait_send()
             for q in range(2 * PIECES):
                 fwd_copy(d, q).wait_send()
@@ -136,6 +149,7 @@
 
         @pl.when(arrived)
         def _():
+            pos_copy(d).wait_recv()
             halo_copy(d).wait_recv()
             for q in range(2 * PIECES):
                 fwd_copy(d, q).wait_recv()
@@ -145,41 +159,47 @@
             hop(k, p).wait_send()
             last(k, p).wait_send()
     centre.wait()
-    first = pltpu.make_async_copy(own_win, own_out, local_sem.at[1])
-    second = pltpu.make_async_copy(partner_win, partner_out, local_sem.at[2])
-    first.start()
-    second.start()
-    first.wait()
-    second.wait()
-
-
-def exchange(own, groups):
+    pos_centre.wait()
+    outs = ((own_win, own_out), (partner_win, partner_out), (pos_win, pos_out))
+    copies = [pltpu.make_async_copy(a, b, local_sem.at[1 + n]) for n, (a, b) in enumerate(outs)]
+    for copy in copies:
+        copy.start()
+    for copy in copies:
+        copy.wait()
+
+
+def exchange(own, positives, groups):
     rows, features = own.shape
+    lanes = 128
+    lined = positives.reshape(rows // lanes, lanes)
     window = jax.ShapeDtypeStruct((3 * rows, features), own.dtype)
+    pos_window = jax.ShapeDtypeStruct((3 * rows // lanes, lanes), jnp.int32)
     anywhere = pl.BlockSpec(memory_space=pl.ANY)
-    return pl.pallas_call(
+    own_win, partner_win, pos_win = pl.pallas_call(
         functools.partial(exchange_kernel, groups),
-        out_shape=(window, window),
-        in_specs=[anywhere],
-        out_specs=(anywhere, anywhere),
+        out_shape=(window, window, pos_window),
+        in_specs=[anywhere, anywhere],
+        out_specs=(anywhere, anywhere, anywhere),
         scratch_shapes=[
             pltpu.VMEM((3 * rows, features), own.dtype),
             pltpu.VMEM((3 * rows, features), own.dtype),
+            pltpu.VMEM((3 * rows // lanes, lanes), jnp.int32),
             pltpu.VMEM((2, rows // 2, features), own.dtype),
-            pltpu.SemaphoreType.DMA((3,)),
+            pltpu.SemaphoreType.DMA((4,)),
             pltpu.SemaphoreType.DMA((2, PIECES)),
             pltpu.SemaphoreType.DMA((2, PIECES)),
             pltpu.SemaphoreType.DMA((2, PIECES)),
             pltpu.SemaphoreType.DMA((2, PIECES)),
             pltpu.SemaphoreType.DMA((2, 2 * PIECES)),
             pltpu.SemaphoreType.DMA((2, 2 * PIECES)),
-            pltpu.SemaphoreType.DMA((2,)),
-            pltpu.SemaphoreType.DMA((2,)),
+            pltpu.SemaphoreType.DMA((4,)),
+            pltpu.SemaphoreType.DMA((4,)),
         ],
         compiler_params=pltpu.CompilerParams(
             collective_id=0, has_side_effects=True, vmem_limit_bytes=32 * 1024 * 1024
         ),
-    )(own)
+    )(own, lined)
+    return own_win, partner_win, pos_win.reshape(3 * rows)
 
 
 def masked_lse(scores, allowed, axis):
@@ -197,9 +217,7 @@
     first_row = me * row_count
     spectral = lax.axis_index("sec") == 0
 
-    own_win, partner_win = exchange(own, lax.axis_size("grp"))
-    pos_left, pos_right = neighbours(positives, ROWS)
-    pos_win = jnp.concatenate([pos_left, positives, pos_right], axis=0)
+    own_win, partner_win, pos_win = exchange(own, positives, lax.axis_size("grp"))
     win = 3 * row_count
 
     padded = jnp.pad(bin_ids, blocks, constant_values=-1)
@@ -222,7 +240,8 @@
     own_index = first_row + jnp.arange(row_count, dtype=jnp.int32)
     spectra_hits = window_index[None, :] == positives[:, None]
     molecule_hits = pos_win[None, :] == own_index[:, None]
-    hits = jnp.where(spectral, spectra_hits, molecule_hits).astype(jnp.float32)
+    hits = jnp.where(spectral, spectra_hits, molecule_hits) & own_allowed
+    hits = hits.astype(jnp.float32)
 
     weights = jnp.exp(own_scores - own_total) + jnp.exp(own_scores - partner_total)
     weights = jnp.where(own_allowed, weights, 0.0) - 2.0 * hits

time: 85.8 us -> 81.5 us (0.950)
  the two profiles are of different devices: /device:TPU:251 before, /device:TPU:255 now
where the time goes in v5:
time: 81.5 us; the launch traced here: 81.3 us
  Pallas kernels  60 us (74%)
  matrix products  11.7 us (14%)
  other arithmetic  5.48 us (7%)
  local copies, waits for them, and re-layouts  3.94 us (5%)
    pallas_call x1, Pallas kernels, exchange(): pl.pallas_call(functools.partial(exchange_kernel, groups), out_shape=(win...  60 us
    dot_general x1, matrix products, local(): jnp.dot(weights.astype(jnp.bfloat16), partner_win, preferred_element_type...  6.12 us
    dot_general x1, matrix products, local(): lax.dot_general(own_win, partner_win, (((1,), (1,)), ((), ())), preferred...  5.63 us
    reduce_sum x2, other arithmetic, masked_lse(): jnp.sum(jnp.where(allowed, jnp.exp(scores - top), 0.0), axis=axis, keepdi...  3.18 us
    unnamed x10, local copies, waits for them, and re-layouts  3.11 us

profile of v5, /device:TPU:255, one launch (start us, length us, event | category | flops | bytes accessed | tf_op | source)
XLA Modules:
  0.0 81.3 jit_solution(5629645557059005967)
XLA Ops:
  0.0 0.8 pad_dynamic-slice_fusion
  0.8 0.1 broadcast_in_dim.45
  0.8 0.0 copy-start
  0.8 1.2 %copy-done = bf16[1,512,1024]{2,1,0:T(8,128)(2,1)S(1)} copy-done((bf16[1,512,1024]{2,1,0:T(8,128)(2,1)S(1)}, bf16[1,512,1024]{2,1,0:T(8,128)(2,1)}, u32[]{:S(2)}) %copy-start) | copy-done | bytes 1048600
  2.1 0.0 copy-start.1
  2.1 0.7 copy-done.1
  2.8 60.0 %shard_map.37 = (bf16[1536,1024]{1,0:T(8,128)(2,1)S(1)}, bf16[1536,1024]{1,0:T(8,128)(2,1)S(1)}, s32[12,128]{1,0:T(8,128)S(1)}) custom-call(bf16[512,1024]{1,0:T(8,128)(2,1)S(1)} %bitcast.8, s32[4,128]{1,0:T(4,128)S(1)} %bitcast.9), custom_call_target="tpu_custom_call" | custom-call | tf_op jit(solution)/shard_map/pallas_call | solution.py:178
  62.8 5.6 %select_reduce_fusion.1 = (f32[1536]{0:T(1024)S(1)}, f32[1536,1536]{1,0:T(8,128)S(1)}) fusion(s32[1536]{0:T(1024)S(1)} %get-tuple-element.12, s32[1536]{0:T(1024)S(1)} %get-tuple-element.11, bf16[1536,1024]{1,0:T(8,128)(2,1)S(1)} %get-tuple-element.8, bf16[1536,1024]{1,0:T(8,128)(2,1)S(1)} %get-tuple-element.9), kind=kOutput, calls=%fused_computation.2 | convolution fusion | flops 4841273856 | bytes 15747072 | tf_op jit(solution)/shard_map/dot_general | solution.py:230
  68.4 0.0 copy-start.3
  68.4 1.6 %broadcast_compare_fusion = pred[1536,1536]{1,0:T(32,128)(4,1)S(1)} fusion(s32[1536]{0:T(1024)S(1)} %get-tuple-element.12, s32[1536]{0:T(1024)S(1)} %get-tuple-element.11), kind=kLoop, calls=%fused_computation.3 | loop fusion | flops 2359296 | bytes 2371584 | tf_op jit(solution)/shard_map/eq | solution.py:228
  70.0 0.0 copy-start.4
  70.0 0.6 select_reduce_fusion.3
  70.7 0.9 %select_reduce_fusion.2 = f32[512]{0:T(512)S(1)} fusion(f32[1536,1536]{1,0:T(8,128)S(1)} %get-tuple-element.14, pred[1536,1536]{1,0:T(32,128)(4,1)S(1)} %broadcast_compare_fusion, f32[512]{0:T(512)S(1)} %is-finite_select_fusion.1), kind=kLoop, calls=%fused_computation.5 | loop fusion | flops 2358784 | bytes 3936256 | tf_op jit(solution)/shard_map/reduce_sum | solution.py:208
  71.6 0.4 copy-done.4
  72.0 0.8 copy-done.3
  72.8 0.0 copy-start.2
  72.8 2.3 %select_reduce_fusion = f32[1536]{0:T(1024)S(1)} fusion(f32[1536,1536]{1,0:T(8,128)S(1)} %get-tuple-element.14, f32[1536]{0:T(1024)S(1)} %is-finite_select_fusion, s32[1536]{0:T(1024)S(1)} %get-tuple-element.12, s32[1536]{0:T(1024)S(1)} %get-tuple-element.11), kind=kLoop, calls=%fused_computation.1 | loop fusion | flops 9435648 | bytes 9461760 | tf_op jit(solution)/shard_map/reduce_sum | solution.py:208
  75.1 0.0 copy-done.2
  75.2 6.1 %fusion.8 = bf16[1,512,1024]{2,1,0:T(8,128)(2,1)} fusion(bf16[1536,1024]{1,0:T(8,128)(2,1)S(1)} %get-tuple-element.9, f32[1536,1536]{1,0:T(8,128)} %copy-done.3, pred[1536,1536]{1,0:T(32,128)(4,1)} %copy-done.4, s32[1536]{0:T(1024)S(1)} %bitcast.10, s32[1536]{0:T(1024)S(1)} %iota_add_fusion, f32[1536]{0:T(1024)S(1)} %log_add_fusion, ...), kind=kOutput, calls=%fused_computation.16 | convolution fusion | flops 1620312064 | bytes 8151041 | tf_op jit(solution)/shard_map/dot_general | solution.py:248
  (8 shorter events, 0.1 us)
Async XLA Ops:
  0.8 1.2 %copy-start = (bf16[1,512,1024]{2,1,0:T(8,128)(2,1)S(1)}, bf16[1,512,1024]{2,1,0:T(8,128)(2,1)}, u32[]{:S(2)}) copy-start(bf16[1,512,1024]{2,1,0:T(8,128)(2,1)} %param.3) | copy-start | bytes 3145732
  2.1 0.7 copy-start.1
  68.4 4.4 %copy-start.3 = (f32[1536,1536]{1,0:T(8,128)}, f32[1536,1536]{1,0:T(8,128)S(1)}, u32[]{:S(2)}) copy-start(f32[1536,1536]{1,0:T(8,128)S(1)} %get-tuple-element.14) | copy-start | bytes 28311556
  70.0 2.0 %copy-start.4 = (pred[1536,1536]{1,0:T(32,128)(4,1)}, pred[1536,1536]{1,0:T(32,128)(4,1)S(1)}, u32[]{:S(2)}) copy-start(pred[1536,1536]{1,0:T(32,128)(4,1)S(1)} %broadcast_compare_fusion) | copy-start | bytes 7077892
  72.8 2.3 %copy-start.2 = (s32[512]{0:T(512)S(1)}, s32[512]{0:T(512)}, u32[]{:S(2)}) copy-start(s32[512]{0:T(512)} %param.5) | copy-start | bytes 6148

commit v6 on v5

v6 whole, which is shorter than its diff:
```python
import functools

import jax
import jax.numpy as jnp
from jax import lax
from jax.experimental import pallas as pl
from jax.experimental.pallas import tpu as pltpu
from jax.sharding import PartitionSpec as P

BLOCK = 256
logit_scale = 0.125
ROWS = ("wide", "grp")


MESH_ID = pl.DeviceIdType.MESH
PIECES = 2
Y_CHIPS = 8


def place_of(groups):
    sec = lax.axis_index("sec")
    wide = lax.axis_index("wide")
    grp = lax.axis_index("grp")
    count = lax.axis_size("wide") * groups
    me = wide * groups + grp
    left_id = (sec, (me - 1) // groups, (me - 1) % groups)
    right_id = (sec, (me + 1) // groups, (me + 1) % groups)
    return sec, wide, grp, me > 0, me < count - 1, left_id, right_id


def greet(peers_always, sides):
    barrier = pltpu.get_barrier_semaphore()
    for peer in peers_always:
        pl.semaphore_signal(barrier, 1, device_id=peer, device_id_type=MESH_ID)
    peers = len(peers_always)
    for present, peer in sides:
        @pl.when(present)
        def _():
            pl.semaphore_signal(barrier, 1, device_id=peer, device_id_type=MESH_ID)

        peers = peers + present.astype(jnp.int32)
    pl.semaphore_wait(barrier, peers)


def exchange_kernel(groups, own_ref, pos_ref, partner_out, pos_out, partner_win, pos_win,
                    relay, local_sem, hop_send, hop_recv, last_send, last_recv, fwd_send,
                    fwd_recv, halo_send, halo_recv):
    rows = own_ref.shape[0]
    half = rows // 2
    piece = half // PIECES
    lines = pos_ref.shape[0]
    sec, wide, grp, has_left, has_right, left_id, right_id = place_of(groups)
    ring = Y_CHIPS
    flipped = jnp.where((wide // ring) % 2 == 0, wide + ring, wide - ring)
    relay_id = ((sec, flipped, grp), (1 - sec, flipped, grp))

    pos_centre = pltpu.make_async_copy(pos_ref, pos_win.at[pl.ds(lines, lines)], local_sem.at[0])
    pos_centre.start()

    for d, arrived in ((0, has_right), (1, has_left)):
        @pl.when(jnp.logical_not(arrived))
        def _():
            place = pl.ds((1 - d) * 2 * rows, rows)
            partner_win[place, :] = jnp.zeros((rows, partner_win.shape[1]), partner_win.dtype)
            pos_win[pl.ds((1 - d) * 2 * lines, lines), :] = jnp.zeros(pos_ref.shape, jnp.int32)

    greet(relay_id, ((has_left, left_id), (has_right, right_id)))

    def hop(k, p):
        return pltpu.make_async_remote_copy(
            src_ref=own_ref.at[pl.ds(k * half + p * piece, piece)],
            dst_ref=relay.at[k, pl.ds(p * piece, piece)],
            send_sem=hop_send.at[k, p], recv_sem=hop_recv.at[k, p],
            device_id=relay_id[k], device_id_type=MESH_ID)

    def last(k, p):
        return pltpu.make_async_remote_copy(
            src_ref=relay.at[k, pl.ds(p * piece, piece)],
            dst_ref=partner_win.at[pl.ds(rows + k * half + p * piece, piece)],
            send_sem=last_send.at[k, p], recv_sem=last_recv.at[k, p],
            device_id=relay_id[1 - k], device_id_type=MESH_ID)

    def pos_copy(d):
        return pltpu.make_async_remote_copy(
            src_ref=pos_ref,
            dst_ref=pos_win.at[pl.ds((1 - d) * 2 * lines, lines)],
            send_sem=halo_send.at[d], recv_sem=halo_recv.at[d],
            device_id=left_id if d == 0 else right_id, device_id_type=MESH_ID)

    def fwd_copy(d, q):
        return pltpu.make_async_remote_copy(
            src_ref=partner_win.at[pl.ds(rows + q * piece, piece)],
            dst_ref=partner_win.at[pl.ds((1 - d) * 2 * rows + q * piece, piece)],
            send_sem=fwd_send.at[d, q], recv_sem=fwd_recv.at[d, q],
            device_id=left_id if d == 0 else right_id, device_id_type=MESH_ID)

    for p in range(PIECES):
        for k in range(2):
            hop(k, p).start()
    sides = ((0, has_left), (1, has_right))
    for d, present in sides:
        @pl.when(present)
        def _():
            pos_copy(d).start()

    for p in range(PIECES):
        for k in range(2):
            hop(k, p).wait_recv()
            last(k, p).start()
    for p in range(PIECES):
        for k in range(2):
            last(k, p).wait_recv()
            q = k * PIECES + p
            for d, present in sides:
                @pl.when(present)
                def _():
                    fwd_copy(d, q).start()

    for d, present in sides:
        @pl.when(present)
        def _():
            pos_copy(d).wait_send()
            for q in range(2 * PIECES):
                fwd_copy(d, q).wait_send()

        arrived = has_right if d == 0 else has_left

        @pl.when(arrived)
        def _():
            pos_copy(d).wait_recv()
            for q in range(2 * PIECES):
                fwd_copy(d, q).wait_recv()

    for p in range(PIECES):
        for k in range(2):
            hop(k, p).wait_send()
            last(k, p).wait_send()
    pos_centre.wait()
    outs = ((partner_win, partner_out), (pos_win, pos_out))
    copies = [pltpu.make_async_copy(a, b, local_sem.at[1 + n]) for n, (a, b) in enumerate(outs)]
    for copy in copies:
        copy.start()
    for copy in copies:
        copy.wait()


def exchange(own, positives, groups):
    rows, features = own.shape
    lanes = 128
    lined = positives.reshape(rows // lanes, lanes)
    window = jax.ShapeDtypeStruct((3 * rows, features), own.dtype)
    pos_window = jax.ShapeDtypeStruct((3 * rows // lanes, lanes), jnp.int32)
    anywhere = pl.BlockSpec(memory_space=pl.ANY)
    partner_win, pos_win = pl.pallas_call(
        functools.partial(exchange_kernel, groups),
        out_shape=(window, pos_window),
        in_specs=[anywhere, anywhere],
        out_specs=(anywhere, anywhere),
        scratch_shapes=[
            pltpu.VMEM((3 * rows, features), own.dtype),
            pltpu.VMEM((3 * rows // lanes, lanes), jnp.int32),
            pltpu.VMEM((2, rows // 2, features), own.dtype),
            pltpu.SemaphoreType.DMA((3,)),
            pltpu.SemaphoreType.DMA((2, PIECES)),
            pltpu.SemaphoreType.DMA((2, PIECES)),
            pltpu.SemaphoreType.DMA((2, PIECES)),
            pltpu.SemaphoreType.DMA((2, PIECES)),
            pltpu.SemaphoreType.DMA((2, 2 * PIECES)),
            pltpu.SemaphoreType.DMA((2, 2 * PIECES)),
            pltpu.SemaphoreType.DMA((2,)),
            pltpu.SemaphoreType.DMA((2,)),
        ],
        compiler_params=pltpu.CompilerParams(
            collective_id=0, has_side_effects=True, vmem_limit_bytes=32 * 1024 * 1024
        ),
    )(own, lined)
    return partner_win, pos_win.reshape(3 * rows)


def partials_kernel(groups, part_ref, out_ref, held, sems):
    lines = part_ref.shape[0]
    third = lines // 3
    sec, wide, grp, has_left, has_right, left_id, right_id = place_of(groups)
    empty = jnp.full((third, part_ref.shape[1]), -jnp.inf, jnp.float32)
    held[0, pl.ds(2 * third, third), :] = empty
    held[1, pl.ds(0, third), :] = empty

    @pl.when(jnp.logical_not(has_left))
    def _():
        held[0, pl.ds(0, 2 * third), :] = jnp.full((2 * third, part_ref.shape[1]), -jnp.inf)

    @pl.when(jnp.logical_not(has_right))
    def _():
        held[1, pl.ds(third, 2 * third), :] = jnp.full((2 * third, part_ref.shape[1]), -jnp.inf)

    greet((), ((has_left, left_id), (has_right, right_id)))

    def send(d):
        return pltpu.make_async_remote_copy(
            src_ref=part_ref.at[pl.ds(d * third, 2 * third)],
            dst_ref=held.at[1 - d, pl.ds((1 - d) * third, 2 * third)],
            send_sem=sems.at[0, d], recv_sem=sems.at[1, d],
            device_id=left_id if d == 0 else right_id, device_id_type=MESH_ID)

    sides = ((0, has_left), (1, has_right))
    for d, present in sides:
        @pl.when(present)
        def _():
            send(d).start()
    for d, present in sides:
        @pl.when(present)
        def _():
            send(d).wait_send()

        arrived = has_right if d == 0 else has_left

        @pl.when(arrived)
        def _():
            send(d).wait_recv()
    out_ref[...] = held[...]


def neighbour_partials(partial, groups):
    lanes = 128
    lined = partial.reshape(-1, lanes)
    held = pl.pallas_call(
        functools.partial(partials_kernel, groups),
        out_shape=jax.ShapeDtypeStruct((2,) + lined.shape, jnp.float32),
        in_specs=[pl.BlockSpec(memory_space=pltpu.VMEM)],
        out_specs=pl.BlockSpec(memory_space=pltpu.VMEM),
        scratch_shapes=[
            pltpu.VMEM((2,) + lined.shape, jnp.float32),
            pltpu.SemaphoreType.DMA((2, 2)),
        ],
        compiler_params=pltpu.CompilerParams(collective_id=1, has_side_effects=True),
    )(lined)
    return held.reshape(2, -1)


def masked_lse(scores, allowed, axis):
    top = jnp.max(jnp.where(allowed, scores, -jnp.inf), axis=axis, keepdims=True)
    top = jnp.where(jnp.isfinite(top), top, 0.0)
    total = jnp.sum(jnp.where(allowed, jnp.exp(scores - top), 0.0), axis=axis, keepdims=True)
    return jnp.log(total) + top


def local(embeddings, bin_ids, positives):
    own = embeddings[0]
    row_count, features = own.shape
    blocks = row_count // BLOCK
    groups = lax.axis_size("grp")
    me = lax.axis_index(ROWS)
    first_row = me * row_count
    spectral = lax.axis_index("sec") == 0

    partner_win, pos_win = exchange(own, positives, groups)
    win = 3 * row_count

    padded = jnp.pad(bin_ids, blocks, constant_values=-1)
    near_bins = jnp.repeat(lax.dynamic_slice_in_dim(padded, me * blocks, 3 * blocks, 0), BLOCK)
    own_bins = jnp.repeat(lax.dynamic_slice_in_dim(bin_ids, me * blocks, blocks, 0), BLOCK)
    allowed = own_bins[:, None] == near_bins[None, :]

    scores = logit_scale * lax.dot_general(
        own, partner_win, (((1,), (1,)), ((), ())), preferred_element_type=jnp.float32
    )
    own_total = masked_lse(scores, allowed, 1)
    partial = masked_lse(scores, allowed, 0)[0]
    beside = neighbour_partials(partial, groups)
    stacked = jnp.stack([partial, beside[0], beside[1]])
    top = jnp.max(stacked, axis=0)
    top = jnp.where(jnp.isfinite(top), top, 0.0)
    partner_total = (jnp.log(jnp.sum(jnp.exp(stacked - top), axis=0)) + top)[None, :]

    window_index = first_row - row_count + jnp.arange(win, dtype=jnp.int32)
    own_index = first_row + jnp.arange(row_count, dtype=jnp.int32)
    spectra_hits = window_index[None, :] == positives[:, None]
    molecule_hits = pos_win[None, :] == own_index[:, None]
    hits = jnp.where(spectral, spectra_hits, molecule_hits) & allowed
    hits = hits.astype(jnp.float32)

    weights = jnp.exp(scores - own_total) + jnp.exp(scores - partner_total)
    weights = jnp.where(allowed, weights, 0.0) - 2.0 * hits
    grad = logit_scale * jnp.dot(
        weights.astype(jnp.bfloat16), partner_win, preferred_element_type=jnp.float32
    )
    return grad.astype(jnp.bfloat16)[None]


def solution(mesh):
    in_specs = (P("sec", ROWS, None), P(), P(ROWS))
    out_specs = P("sec", ROWS, None)
    return jax.shard_map(local, mesh=mesh, in_specs=in_specs, out_specs=out_specs, check_vma=False)
```

time: 81.5 us -> 72.5 us (0.89)
  the two profiles are of different devices: /device:TPU:255 before, /device:TPU:251 now
where the time goes in v6:
time: 72.5 us; the launch traced here: 72 us
  Pallas kernels  55.5 us (77%)
  matrix products  7.89 us (11%)
  local copies, waits for them, and re-layouts  4.31 us (6%)
  other arithmetic  4.21 us (6%)
    pallas_call x1, Pallas kernels, exchange(): pl.pallas_call(functools.partial(exchange_kernel, groups), out_shape=(win...  46.2 us
    pallas_call x1, Pallas kernels, neighbour_partials(): pl.pallas_call(functools.partial(partials_kernel, groups), out_shape=jax....  9.27 us
    dot_general x1, matrix products, local(): jnp.dot(weights.astype(jnp.bfloat16), partner_win, preferred_element_type...  5.88 us
    reduce_sum x2, other arithmetic, masked_lse(): jnp.sum(jnp.where(allowed, jnp.exp(scores - top), 0.0), axis=axis, keepdi...  2.79 us
    unnamed x11, local copies, waits for them, and re-layouts  2.71 us
    dot_general x1, matrix products, local(): lax.dot_general(own, partner_win, (((1,), (1,)), ((), ())), preferred_ele...  2.01 us

profile of v6, /device:TPU:251, one launch (start us, length us, event | category | flops | bytes accessed | tf_op | source)
XLA Modules:
  0.0 72.0 jit_solution(7184014153807089978)
XLA Ops:
  0.0 0.8 %pad_dynamic-slice_fusion = s32[6]{0:T(128)S(1)} fusion(s32[]{:T(128)S(6)} %select_n.76, s32[512]{0:T(512)} %param.4), kind=kLoop, calls=%fused_computation.43 | loop fusion | bytes 2076 | tf_op jit(solution)/shard_map/dynamic_slice | solution.py:260
  0.8 0.8 %dynamic_slice.6 = s32[2]{0:T(128)S(1)} dynamic-slice(s32[512]{0:T(512)} %param.4, s32[]{:T(128)S(6)} %select_n.75), dynamic_slice_sizes={2} | dynamic-slice | bytes 20 | tf_op jit(solution)/shard_map/dynamic_slice | solution.py:261
  1.5 0.1 broadcast_bitcast_fusion
  1.6 0.1 broadcast_in_dim.43
  1.7 0.0 copy-start
  1.7 1.2 %copy-done = bf16[1,512,1024]{2,1,0:T(8,128)(2,1)S(1)} copy-done((bf16[1,512,1024]{2,1,0:T(8,128)(2,1)S(1)}, bf16[1,512,1024]{2,1,0:T(8,128)(2,1)}, u32[]{:S(2)}) %copy-start) | copy-done | bytes 1048600
  2.9 0.0 copy-start.1
  2.9 0.7 copy-done.1
  3.6 46.2 %shard_map.37 = (bf16[1536,1024]{1,0:T(8,128)(2,1)S(1)}, s32[12,128]{1,0:T(8,128)S(1)}) custom-call(bf16[512,1024]{1,0:T(8,128)(2,1)S(1)} %bitcast.36, s32[4,128]{1,0:T(4,128)S(1)} %bitcast.37), custom_call_target="tpu_custom_call" | custom-call | tf_op jit(solution)/shard_map/pallas_call | solution.py:154
  49.8 2.0 %fusion.6 = (f32[512]{0:T(512)S(1)}, f32[512,1536]{0,1:T(8,128)S(1)}) fusion(s32[512]{0:T(512)S(1)} %bitcast.39, s32[1536]{0:T(1024)S(1)} %eq.50, bf16[1536,1024]{1,0:T(8,128)(2,1)S(1)} %get-tuple-element.7, bf16[1,512,1024]{2,1,0:T(8,128)(2,1)S(1)} %copy-done), kind=kOutput, calls=%fused_computation.12 | convolution fusion | flops 1613757952 | bytes 7350272 | tf_op jit(solution)/shard_map/dot_general | solution.py:264
  51.8 0.0 copy-start.3
  51.8 0.0 copy-start.2
  51.8 1.6 %fusion.1 = (f32[512]{0:T(512)S(1)}, f32[1536]{0:T(1024)S(1)}) fusion(f32[512,1536]{0,1:T(8,128)S(1)} %get-tuple-element.16, f32[512]{0:T(512)S(1)} %is-finite_select_fusion.4, s32[512]{0:T(512)S(1)} %bitcast.40, s32[1536]{0:T(1024)S(1)} %eq.50), kind=kLoop, calls=%fused_computation.7 | loop fusion | flops 4716544 | bytes 3164160 | tf_op jit(solution)/shard_map/reduce_sum | solution.py:243
  53.4 1.2 %fusion.2 = f32[1536]{0:T(1024)S(1)} fusion(f32[512,1536]{0,1:T(8,128)S(1)} %get-tuple-element.16, f32[1536]{0:T(1024)S(1)} %is-finite_select_fusion.3, s32[512]{0:T(512)S(1)} %bitcast.41, s32[1536]{0:T(1024)S(1)} %eq.50), kind=kLoop, calls=%fused_computation.8 | loop fusion | flops 3144192 | bytes 3166208 | tf_op jit(solution)/shard_map/reduce_sum | solution.py:243
  54.7 0.0 copy-done.3
  54.7 0.6 fusion.23.part_ref
  55.3 9.3 %shard_map.38 = f32[2,12,128]{2,1,0:T(8,128)} custom-call(f32[12,128]{1,0:T(8,128)} %fusion.23.part_ref), custom_call_target="tpu_custom_call" | custom-call | tf_op jit(solution)/shard_map/pallas_call | solution.py:226
  64.6 0.7 %fusion.28 = (f32[1536]{0:T(1024)S(1)}, f32[1536]{0:T(1024)S(1)}) fusion(f32[1536]{0:T(1024)S(1)} %fusion.2, f32[2,12,128]{2,1,0:T(8,128)} %shard_map.38, f32[1536]{0:T(1024)S(1)} %get-tuple-element.10), kind=kLoop, calls=%fused_computation.50 | loop fusion | flops 10752 | bytes 36864 | tf_op jit(solution)/shard_map/log | solution.py:244
  65.3 0.7 slice_bitcast_fusion.1
  66.1 0.0 copy-done.2
  66.1 5.9 %fusion.18 = bf16[1,512,1024]{2,1,0:T(8,128)(2,1)} fusion(bf16[1536,1024]{1,0:T(8,128)(2,1)S(1)} %get-tuple-element.7, f32[512,1536]{0,1:T(8,128)} %copy-done.3, s32[512]{0:T(512)S(1)} %iota_add_fusion.1, s32[512]{0:T(512)S(1)} %copy-done.2, f32[1536]{0:T(1024)S(1)} %log_add_fusion, f32[512]{0:T(512)S(1)} %log_add_fusion.1, s32[512]{0:T(512)S(1)} %bitcast.42, ...), kind=kOutput, calls=%fused_computation.24 | convolution fusion | flops 1621098496 | bytes 7372801 | tf_op jit(solution)/shard_map/dot_general | solution.py:284
  (11 shorter events, 0.1 us)
Async XLA Ops:
  1.7 1.2 %copy-start = (bf16[1,512,1024]{2,1,0:T(8,128)(2,1)S(1)}, bf16[1,512,1024]{2,1,0:T(8,128)(2,1)}, u32[]{:S(2)}) copy-start(bf16[1,512,1024]{2,1,0:T(8,128)(2,1)} %param.3) | copy-start | bytes 3145732
  2.9 0.7 copy-start.1
  51.8 2.9 %copy-start.3 = (f32[512,1536]{0,1:T(8,128)}, f32[512,1536]{0,1:T(8,128)S(1)}, u32[]{:S(2)}) copy-start(f32[512,1536]{0,1:T(8,128)S(1)} %get-tuple-element.16) | copy-start | bytes 9437188
  51.8 14.3 %copy-start.2 = (s32[512]{0:T(512)S(1)}, s32[512]{0:T(512)}, u32[]{:S(2)}) copy-start(s32[512]{0:T(512)} %param.5) | copy-start | bytes 6148

commit v7 on v6

v7 whole, which is shorter than its diff:
```python
import functools

import jax
import jax.numpy as jnp
from jax import lax
from jax.experimental import pallas as pl
from jax.experimental.pallas import tpu as pltpu
from jax.sharding import PartitionSpec as P

BLOCK = 256
logit_scale = 0.125
ROWS = ("wide", "grp")


MESH_ID = pl.DeviceIdType.MESH
PIECES = 8
IN_FLIGHT = 2


def place_of(groups):
    sec = lax.axis_index("sec")
    wide = lax.axis_index("wide")
    grp = lax.axis_index("grp")
    count = lax.axis_size("wide") * groups
    me = wide * groups + grp
    left_id = (sec, (me - 1) // groups, (me - 1) % groups)
    right_id = (sec, (me + 1) // groups, (me + 1) % groups)
    return sec, wide, grp, me > 0, me < count - 1, left_id, right_id


def greet(peers_always, sides):
    barrier = pltpu.get_barrier_semaphore()
    for peer in peers_always:
        pl.semaphore_signal(barrier, 1, device_id=peer, device_id_type=MESH_ID)
    peers = len(peers_always)
    for present, peer in sides:
        @pl.when(present)
        def _():
            pl.semaphore_signal(barrier, 1, device_id=peer, device_id_type=MESH_ID)

        peers = peers + present.astype(jnp.int32)
    pl.semaphore_wait(barrier, peers)


def exchange_kernel(groups, own_ref, pos_ref, own_bins_ref, near_bins_ref, partner_out, pos_out,
                    own_total_ref, partner_total_ref, partner_win, pos_win, own_rows, partial,
                    held, local_sem, sec_send, sec_recv, fwd_send, fwd_recv, halo_send, halo_recv,
                    part_sems):
    rows = own_ref.shape[0]
    piece = rows // PIECES
    lines = pos_ref.shape[0]
    sec, wide, grp, has_left, has_right, left_id, right_id = place_of(groups)
    partner_id = (1 - sec, wide, grp)

    pos_centre = pltpu.make_async_copy(pos_ref, pos_win.at[pl.ds(lines, lines)], local_sem.at[0])
    pos_centre.start()
    own_copy = pltpu.make_async_copy(own_ref, own_rows, local_sem.at[3])
    own_copy.start()
    win = 3 * rows
    empty = jnp.full((1, rows), -jnp.inf, jnp.float32)
    held[0, :, pl.ds(2 * rows, rows)] = empty
    held[1, :, pl.ds(0, rows)] = empty

    @pl.when(jnp.logical_not(has_left))
    def _():
        held[0, :, pl.ds(0, 2 * rows)] = jnp.full((1, 2 * rows), -jnp.inf, jnp.float32)

    @pl.when(jnp.logical_not(has_right))
    def _():
        held[1, :, pl.ds(rows, 2 * rows)] = jnp.full((1, 2 * rows), -jnp.inf, jnp.float32)

    for d, arrived in ((0, has_right), (1, has_left)):
        @pl.when(jnp.logical_not(arrived))
        def _():
            place = pl.ds((1 - d) * 2 * rows, rows)
            partner_win[place, :] = jnp.zeros((rows, partner_win.shape[1]), partner_win.dtype)
            pos_win[pl.ds((1 - d) * 2 * lines, lines), :] = jnp.zeros(pos_ref.shape, jnp.int32)

    greet((partner_id,), ((has_left, left_id), (has_right, right_id)))

    def sec_copy(q):
        return pltpu.make_async_remote_copy(
            src_ref=own_ref.at[pl.ds(q * piece, piece)],
            dst_ref=partner_win.at[pl.ds(rows + q * piece, piece)],
            send_sem=sec_send.at[q], recv_sem=sec_recv.at[q],
            device_id=partner_id, device_id_type=MESH_ID)

    def pos_copy(d):
        return pltpu.make_async_remote_copy(
            src_ref=pos_ref,
            dst_ref=pos_win.at[pl.ds((1 - d) * 2 * lines, lines)],
            send_sem=halo_send.at[d], recv_sem=halo_recv.at[d],
            device_id=left_id if d == 0 else right_id, device_id_type=MESH_ID)

    def fwd_copy(d, q):
        return pltpu.make_async_remote_copy(
            src_ref=partner_win.at[pl.ds(rows + q * piece, piece)],
            dst_ref=partner_win.at[pl.ds((1 - d) * 2 * rows + q * piece, piece)],
            send_sem=fwd_send.at[d, q], recv_sem=fwd_recv.at[d, q],
            device_id=left_id if d == 0 else right_id, device_id_type=MESH_ID)

    sides = ((0, has_left), (1, has_right))
    for d, present in sides:
        @pl.when(present)
        def _():
            pos_copy(d).start()

    for q in range(IN_FLIGHT):
        sec_copy(q).start()
    for q in range(PIECES):
        sec_copy(q).wait_send()
        if q + IN_FLIGHT < PIECES:
            sec_copy(q + IN_FLIGHT).start()
        sec_copy(q).wait_recv()
        for d, present in sides:
            @pl.when(present)
            def _():
                fwd_copy(d, q).start()

    for d, present in sides:
        @pl.when(present)
        def _():
            pos_copy(d).wait_send()
            for q in range(PIECES):
                fwd_copy(d, q).wait_send()

        arrived = has_right if d == 0 else has_left

        @pl.when(arrived)
        def _():
            pos_copy(d).wait_recv()
            for q in range(PIECES):
                fwd_copy(d, q).wait_recv()

    pos_centre.wait()
    outs = ((partner_win, partner_out), (pos_win, pos_out))
    copies = [pltpu.make_async_copy(a, b, local_sem.at[1 + n]) for n, (a, b) in enumerate(outs)]
    for copy in copies:
        copy.start()

    own_copy.wait()
    scores = logit_scale * lax.dot_general(
        own_rows[...], partner_win[...], (((1,), (1,)), ((), ())),
        preferred_element_type=jnp.float32,
    )
    allowed = own_bins_ref[...] == near_bins_ref[...]
    own_total_ref[...] = masked_lse(scores, allowed, 1)
    partial[...] = masked_lse(scores, allowed, 0)

    def part_copy(d):
        return pltpu.make_async_remote_copy(
            src_ref=partial.at[:, pl.ds(d * rows, 2 * rows)],
            dst_ref=held.at[1 - d, :, pl.ds((1 - d) * rows, 2 * rows)],
            send_sem=part_sems.at[0, d], recv_sem=part_sems.at[1, d],
            device_id=left_id if d == 0 else right_id, device_id_type=MESH_ID)

    for d, present in sides:
        @pl.when(present)
        def _():
            part_copy(d).start()
    for d, present in sides:
        @pl.when(present)
        def _():
            part_copy(d).wait_send()

        arrived = has_right if d == 0 else has_left

        @pl.when(arrived)
        def _():
            part_copy(d).wait_recv()

    mine, left, right = partial[...], held[0], held[1]
    top = jnp.maximum(jnp.maximum(mine, left), right)
    top = jnp.where(top > -jnp.inf, top, 0.0)
    total = jnp.exp(mine - top) + jnp.exp(left - top) + jnp.exp(right - top)
    partner_total_ref[...] = jnp.log(total) + top
    for copy in copies:
        copy.wait()


def exchange(own, positives, own_bins, near_bins, groups):
    rows, features = own.shape
    lanes = 128
    lined = positives.reshape(rows // lanes, lanes)
    window = jax.ShapeDtypeStruct((3 * rows, features), own.dtype)
    pos_window = jax.ShapeDtypeStruct((3 * rows // lanes, lanes), jnp.int32)
    own_total = jax.ShapeDtypeStruct((rows, 1), jnp.float32)
    partner_total = jax.ShapeDtypeStruct((1, 3 * rows), jnp.float32)
    anywhere = pl.BlockSpec(memory_space=pl.ANY)
    vmem = pl.BlockSpec(memory_space=pltpu.VMEM)
    partner_win, pos_win, own_total, partner_total = pl.pallas_call(
        functools.partial(exchange_kernel, groups),
        out_shape=(window, pos_window, own_total, partner_total),
        in_specs=[anywhere, anywhere, vmem, vmem],
        out_specs=(anywhere, anywhere, vmem, vmem),
        scratch_shapes=[
            pltpu.VMEM((3 * rows, features), own.dtype),
            pltpu.VMEM((3 * rows // lanes, lanes), jnp.int32),
            pltpu.VMEM((rows, features), own.dtype),
            pltpu.VMEM((1, 3 * rows), jnp.float32),
            pltpu.VMEM((2, 1, 3 * rows), jnp.float32),
            pltpu.SemaphoreType.DMA((4,)),
            pltpu.SemaphoreType.DMA((PIECES,)),
            pltpu.SemaphoreType.DMA((PIECES,)),
            pltpu.SemaphoreType.DMA((2, PIECES)),
            pltpu.SemaphoreType.DMA((2, PIECES)),
            pltpu.SemaphoreType.DMA((2,)),
            pltpu.SemaphoreType.DMA((2,)),
            pltpu.SemaphoreType.DMA((2, 2)),
        ],
        compiler_params=pltpu.CompilerParams(
            collective_id=0, has_side_effects=True, vmem_limit_bytes=48 * 1024 * 1024
        ),
    )(own, lined, own_bins, near_bins)
    return partner_win, pos_win.reshape(3 * rows), own_total, partner_total


def masked_lse(scores, allowed, axis):
    top = jnp.max(jnp.where(allowed, scores, -jnp.inf), axis=axis, keepdims=True)
    top = jnp.where(top > -jnp.inf, top, 0.0)
    total = jnp.sum(jnp.where(allowed, jnp.exp(scores - top), 0.0), axis=axis, keepdims=True)
    return jnp.log(total) + top


def local(embeddings, bin_ids, positives):
    own = embeddings[0]
    row_count, features = own.shape
    blocks = row_count // BLOCK
    groups = lax.axis_size("grp")
    me = lax.axis_index(ROWS)
    first_row = me * row_count
    spectral = lax.axis_index("sec") == 0

    win = 3 * row_count

    padded = jnp.pad(bin_ids, blocks, constant_values=-1)
    near_bins = jnp.repeat(lax.dynamic_slice_in_dim(padded, me * blocks, 3 * blocks, 0), BLOCK)
    own_bins = jnp.repeat(lax.dynamic_slice_in_dim(bin_ids, me * blocks, blocks, 0), BLOCK)
    own_bins = own_bins[:, None]
    near_bins = near_bins[None, :]
    partner_win, pos_win, own_total, partner_total = exchange(
        own, positives, own_bins, near_bins, groups
    )

    window_index = first_row - row_count + jnp.arange(win, dtype=jnp.int32)
    own_index = first_row + jnp.arange(row_count, dtype=jnp.int32)
    spectra_hits = window_index[None, :] == positives[:, None]
    molecule_hits = pos_win[None, :] == own_index[:, None]
    allowed = own_bins == near_bins
    hits = jnp.where(spectral, spectra_hits, molecule_hits) & allowed
    hits = hits.astype(jnp.float32)

    scores = logit_scale * lax.dot_general(
        own, partner_win, (((1,), (1,)), ((), ())), preferred_element_type=jnp.float32
    )
    weights = jnp.exp(scores - own_total) + jnp.exp(scores - partner_total)
    weights = jnp.where(allowed, weights, 0.0) - 2.0 * hits
    grad = logit_scale * jnp.dot(
        weights.astype(jnp.bfloat16), partner_win, preferred_element_type=jnp.float32
    )
    return grad.astype(jnp.bfloat16)[None]


def solution(mesh):
    in_specs = (P("sec", ROWS, None), P(), P(ROWS))
    out_specs = P("sec", ROWS, None)
    return jax.shard_map(local, mesh=mesh, in_specs=in_specs, out_specs=out_specs, check_vma=False)
```

time: 72.5 us -> 69 us (0.952)
  the two profiles are of different devices: /device:TPU:251 before, /device:TPU:256 now
where the time goes in v7:
time: 69 us; the launch traced here: 68.8 us
  Pallas kernels  54.2 us (79%)
  matrix products  8.97 us (13%)
  local copies, waits for them, and re-layouts  5.45 us (8%)
    pallas_call x1, Pallas kernels, exchange(): pl.pallas_call(functools.partial(exchange_kernel, groups), out_shape=(win...  54.2 us
    dot_general x1, matrix products, local(): jnp.dot(weights.astype(jnp.bfloat16), partner_win, preferred_element_type...  8.97 us
    unnamed x12, local copies, waits for them, and re-layouts  3.86 us

profile of v7, /device:TPU:256, one launch (start us, length us, event | category | flops | bytes accessed | tf_op | source)
XLA Modules:
  0.0 68.8 jit_solution(5759137849570668760)
XLA Ops:
  0.0 0.8 %pad_dynamic-slice_fusion = s32[6]{0:T(128)S(1)} fusion(s32[]{:T(128)S(6)} %select_n.19, s32[512]{0:T(512)} %param.4), kind=kLoop, calls=%fused_computation.9 | loop fusion | bytes 2076 | tf_op jit(solution)/shard_map/dynamic_slice | solution.py:237
  0.8 0.8 %dynamic_slice.6 = s32[2]{0:T(128)S(1)} dynamic-slice(s32[512]{0:T(512)} %param.4, s32[]{:T(128)S(6)} %select_n.18), dynamic_slice_sizes={2} | dynamic-slice | bytes 20 | tf_op jit(solution)/shard_map/dynamic_slice | solution.py:238
  1.5 0.1 broadcast_bitcast_fusion.2
  1.6 0.1 broadcast_bitcast_fusion
  1.7 0.1 broadcast_in_dim.17
  1.8 0.1 copy.7
  1.9 0.0 copy-start
  1.9 1.2 %copy-done = bf16[1,512,1024]{2,1,0:T(8,128)(2,1)S(1)} copy-done((bf16[1,512,1024]{2,1,0:T(8,128)(2,1)S(1)}, bf16[1,512,1024]{2,1,0:T(8,128)(2,1)}, u32[]{:S(2)}) %copy-start) | copy-done | bytes 1048600
  3.1 0.0 copy-start.1
  3.1 0.7 copy-done.1
  3.8 54.2 %shard_map.37 = (bf16[1536,1024]{1,0:T(8,128)(2,1)S(1)}, s32[12,128]{1,0:T(8,128)S(1)}, f32[512,1]{1,0:T(8,128)S(1)}, f32[1,1536]{1,0:T(1,128)S(1)}) custom-call(bf16[512,1024]{1,0:T(8,128)(2,1)S(1)} %bitcast.26, s32[4,128]{1,0:T(4,128)S(1)} %bitcast.29, s32[512,1]{1,0:T(8,128)S(1)} %bitcast.27, s32[1,1536]{1,0:T(1,128)S(1)} %bitcast.28), custom_call_target="tpu_custom_call" | custom-call | tf_op jit(solution)/shard_map/pallas_call | solution.py:191
  58.0 0.0 copy-start.2
  58.0 1.7 %copy-done.2 = bf16[1536,1024]{1,0:T(8,128)(2,1)} copy-done((bf16[1536,1024]{1,0:T(8,128)(2,1)}, bf16[1536,1024]{1,0:T(8,128)(2,1)S(1)}, u32[]{:S(2)}) %copy-start.2) | copy-done | bytes 3145752
  59.7 0.1 reduce
  59.8 9.0 %fusion.2 = bf16[1,512,1024]{2,1,0:T(8,128)(2,1)} fusion(bf16[1536,1024]{1,0:T(8,128)(2,1)} %copy-done.2, s32[512]{0:T(512)S(1)} %iota_add_fusion.1, s32[512]{0:T(512)} %param.5, f32[1536]{0:T(1024)S(1)} %reduce.1, f32[512]{0:T(512)S(1)} %reduce, s32[512]{0:T(512)S(1)} %bitcast.32, s32[1536]{0:T(1024)S(1)} %bitcast.30, s32[1536]{0:T(1024)S(1)} %iota_add_fusion, ...), kind=kOutput, calls=%fused_computation.6 | convolution fusion | flops 3232497664 | bytes 5275649 | tf_op jit(solution)/shard_map/dot_general | solution.py:258
  (7 shorter events, 0.1 us)
Async XLA Ops:
  1.9 1.2 %copy-start = (bf16[1,512,1024]{2,1,0:T(8,128)(2,1)S(1)}, bf16[1,512,1024]{2,1,0:T(8,128)(2,1)}, u32[]{:S(2)}) copy-start(bf16[1,512,1024]{2,1,0:T(8,128)(2,1)} %param.3) | copy-start | bytes 3145732
  3.1 0.7 copy-start.1
  58.0 1.7 %copy-start.2 = (bf16[1536,1024]{1,0:T(8,128)(2,1)}, bf16[1536,1024]{1,0:T(8,128)(2,1)S(1)}, u32[]{:S(2)}) copy-start(bf16[1536,1024]{1,0:T(8,128)(2,1)S(1)} %get-tuple-element.9) | copy-start | bytes 9437188

commit v8 on v7

--- a/solution.py
+++ b/solution.py
@@ -42,18 +42,16 @@
     pl.semaphore_wait(barrier, peers)
 
 
-def exchange_kernel(groups, own_ref, pos_ref, own_bins_ref, near_bins_ref, partner_out, pos_out,
-                    own_total_ref, partner_total_ref, partner_win, pos_win, own_rows, partial,
-                    held, local_sem, sec_send, sec_recv, fwd_send, fwd_recv, halo_send, halo_recv,
+def exchange_kernel(groups, own_ref, pos_ref, own_bins_ref, near_bins_ref, row_key_ref,
+                    window_key_ref, grad_ref, partner_win, pos_win, own_rows, partial, held,
+                    local_sem, sec_send, sec_recv, fwd_send, fwd_recv, halo_send, halo_recv,
                     part_sems):
     rows = own_ref.shape[0]
     piece = rows // PIECES
-    lines = pos_ref.shape[0]
     sec, wide, grp, has_left, has_right, left_id, right_id = place_of(groups)
     partner_id = (1 - sec, wide, grp)
 
-    pos_centre = pltpu.make_async_copy(pos_ref, pos_win.at[pl.ds(lines, lines)], local_sem.at[0])
-    pos_centre.start()
+    pos_win[:, pl.ds(rows, rows)] = pos_ref[...]
     own_copy = pltpu.make_async_copy(own_ref, own_rows, local_sem.at[3])
     own_copy.start()
     win = 3 * rows
@@ -74,7 +72,7 @@
         def _():
             place = pl.ds((1 - d) * 2 * rows, rows)
             partner_win[place, :] = jnp.zeros((rows, partner_win.shape[1]), partner_win.dtype)
-            pos_win[pl.ds((1 - d) * 2 * lines, lines), :] = jnp.zeros(pos_ref.shape, jnp.int32)
+            pos_win[:, pl.ds((1 - d) * 2 * rows, rows)] = jnp.zeros(pos_ref.shape, jnp.int32)
 
     greet((partner_id,), ((has_left, left_id), (has_right, right_id)))
 
@@ -88,7 +86,7 @@
     def pos_copy(d):
         return pltpu.make_async_remote_copy(
             src_ref=pos_ref,
-            dst_ref=pos_win.at[pl.ds((1 - d) * 2 * lines, lines)],
+            dst_ref=pos_win.at[:, pl.ds((1 - d) * 2 * rows, rows)],
             send_sem=halo_send.at[d], recv_sem=halo_recv.at[d],
             device_id=left_id if d == 0 else right_id, device_id_type=MESH_ID)
 
@@ -132,19 +130,13 @@
             for q in range(PIECES):
                 fwd_copy(d, q).wait_recv()
 
-    pos_centre.wait()
-    outs = ((partner_win, partner_out), (pos_win, pos_out))
-    copies = [pltpu.make_async_copy(a, b, local_sem.at[1 + n]) for n, (a, b) in enumerate(outs)]
-    for copy in copies:
-        copy.start()
-
     own_copy.wait()
     scores = logit_scale * lax.dot_general(
         own_rows[...], partner_win[...], (((1,), (1,)), ((), ())),
         preferred_element_type=jnp.float32,
     )
     allowed = own_bins_ref[...] == near_bins_ref[...]
-    own_total_ref[...] = masked_lse(scores, allowed, 1)
+    own_total = masked_lse(scores, allowed, 1)
     partial[...] = masked_lse(scores, allowed, 0)
 
     def part_copy(d):
@@ -173,29 +165,28 @@
     top = jnp.maximum(jnp.maximum(mine, left), right)
     top = jnp.where(top > -jnp.inf, top, 0.0)
     total = jnp.exp(mine - top) + jnp.exp(left - top) + jnp.exp(right - top)
-    partner_total_ref[...] = jnp.log(total) + top
-    for copy in copies:
-        copy.wait()
-
-
-def exchange(own, positives, own_bins, near_bins, groups):
+    partner_total = jnp.log(total) + top
+
+    col_key = jnp.where(sec == 0, window_key_ref[...], pos_win[...])
+    hits = allowed & (row_key_ref[...] == col_key)
+    weights = jnp.exp(scores - own_total) + jnp.exp(scores - partner_total)
+    weights = jnp.where(allowed, weights, 0.0) - jnp.where(hits, 2.0, 0.0)
+    grad = jnp.dot(weights.astype(jnp.bfloat16), partner_win[...], preferred_element_type=jnp.float32)
+    grad_ref[...] = (logit_scale * grad).astype(grad_ref.dtype)
+
+
+def exchange(own, positives, own_bins, near_bins, row_key, window_key, groups):
     rows, features = own.shape
-    lanes = 128
-    lined = positives.reshape(rows // lanes, lanes)
-    window = jax.ShapeDtypeStruct((3 * rows, features), own.dtype)
-    pos_window = jax.ShapeDtypeStruct((3 * rows // lanes, lanes), jnp.int32)
-    own_total = jax.ShapeDtypeStruct((rows, 1), jnp.float32)
-    partner_total = jax.ShapeDtypeStruct((1, 3 * rows), jnp.float32)
     anywhere = pl.BlockSpec(memory_space=pl.ANY)
     vmem = pl.BlockSpec(memory_space=pltpu.VMEM)
-    partner_win, pos_win, own_total, partner_total = pl.pallas_call(
+    return pl.pallas_call(
         functools.partial(exchange_kernel, groups),
-        out_shape=(window, pos_window, own_total, partner_total),
-        in_specs=[anywhere, anywhere, vmem, vmem],
-        out_specs=(anywhere, anywhere, vmem, vmem),
+        out_shape=jax.ShapeDtypeStruct((rows, features), own.dtype),
+        in_specs=[anywhere] + [vmem] * 5,
+        out_specs=vmem,
         scratch_shapes=[
             pltpu.VMEM((3 * rows, features), own.dtype),
-            pltpu.VMEM((3 * rows // lanes, lanes), jnp.int32),
+            pltpu.VMEM((1, 3 * rows), jnp.int32),
             pltpu.VMEM((rows, features), own.dtype),
             pltpu.VMEM((1, 3 * rows), jnp.float32),
             pltpu.VMEM((2, 1, 3 * rows), jnp.float32),
@@ -211,8 +202,7 @@
         compiler_params=pltpu.CompilerParams(
             collective_id=0, has_side_effects=True, vmem_limit_bytes=48 * 1024 * 1024
         ),
-    )(own, lined, own_bins, near_bins)
-    return partner_win, pos_win.reshape(3 * rows), own_total, partner_total
+    )(own, positives[None, :], own_bins, near_bins, row_key, window_key)
 
 
 def masked_lse(scores, allowed, axis):
@@ -238,27 +228,11 @@
     own_bins = jnp.repeat(lax.dynamic_slice_in_dim(bin_ids, me * blocks, blocks, 0), BLOCK)
     own_bins = own_bins[:, None]
     near_bins = near_bins[None, :]
-    partner_win, pos_win, own_total, partner_total = exchange(
-        own, positives, own_bins, near_bins, groups
-    )
-
     window_index = first_row - row_count + jnp.arange(win, dtype=jnp.int32)
     own_index = first_row + jnp.arange(row_count, dtype=jnp.int32)
-    spectra_hits = window_index[None, :] == positives[:, None]
-    molecule_hits = pos_win[None, :] == own_index[:, None]
-    allowed = own_bins == near_bins
-    hits = jnp.where(spectral, spectra_hits, molecule_hits) & allowed
-    hits = hits.astype(jnp.float32)
-
-    scores = logit_scale * lax.dot_general(
-        own, partner_win, (((1,), (1,)), ((), ())), preferred_element_type=jnp.float32
-    )
-    weights = jnp.exp(scores - own_total) + jnp.exp(scores - partner_total)
-    weights = jnp.where(allowed, weights, 0.0) - 2.0 * hits
-    grad = logit_scale * jnp.dot(
-        weights.astype(jnp.bfloat16), partner_win, preferred_element_type=jnp.float32
-    )
-    return grad.astype(jnp.bfloat16)[None]
+    row_key = jnp.where(spectral, positives, own_index)[:, None]
+    grad = exchange(own, positives, own_bins, near_bins, row_key, window_index[None, :], groups)
+    return grad[None]
 
 
 def solution(mesh):

time: 69 us -> 61.2 us (0.89)
  matrix products: 8.97 us -> 0 us
  Pallas kernels: 54.2 us -> 56.7 us
  local copies, waits for them, and re-layouts: 5.45 us -> 4.16 us
    dot_general x1 -> x0, matrix products: 8.97 us -> none  [local(): jnp.dot(weights.astype(jnp.bfloat16), partner_win, preferred_element_type...]
    pallas_call x1, Pallas kernels: 54.2 us -> 56.7 us  [exchange(): pl.pallas_call(functools.partial(exchange_kernel, groups), out_shape=jax....]
where the time goes in v8:
time: 61.2 us; the launch traced here: 61 us
  Pallas kernels  56.7 us (93%)
  local copies, waits for them, and re-layouts  4.16 us (7%)
    pallas_call x1, Pallas kernels, exchange(): pl.pallas_call(functools.partial(exchange_kernel, groups), out_shape=jax....  56.7 us
    unnamed x12, local copies, waits for them, and re-layouts  3.86 us

profile of v8, /device:TPU:256, one launch (start us, length us, event | category | flops | bytes accessed | tf_op | source)
XLA Modules:
  0.0 61.0 jit_solution(10669195419012404671)
XLA Ops:
  0.0 0.0 copy-start.2
  0.0 0.7 %copy-done.2 = s32[512]{0:T(512)S(1)} copy-done((s32[512]{0:T(512)S(1)}, s32[512]{0:T(512)}, u32[]{:S(2)}) %copy-start.2) | copy-done | bytes 2072
  0.7 0.1 pad_dynamic-slice_fusion
  0.8 0.1 dynamic_slice.6
  0.8 0.0 copy-start.1
  0.8 0.7 %copy-done.1 = s32[512]{0:T(512)S(1)} copy-done((s32[512]{0:T(512)S(1)}, s32[512]{0:T(512)}, u32[]{:S(2)}) %copy-start.1) | copy-done | bytes 2072
  1.5 0.1 broadcast_bitcast_fusion.1
  1.6 0.1 broadcast_bitcast_fusion
  1.7 0.1 copy.7
  1.8 0.1 copy.5.row_key_ref
  2.0 0.0 copy-start
  2.0 1.2 %copy-done = bf16[1,512,1024]{2,1,0:T(8,128)(2,1)S(1)} copy-done((bf16[1,512,1024]{2,1,0:T(8,128)(2,1)S(1)}, bf16[1,512,1024]{2,1,0:T(8,128)(2,1)}, u32[]{:S(2)}) %copy-start) | copy-done | bytes 1048600
  3.2 56.7 %shard_map.37 = bf16[512,1024]{1,0:T(8,128)(2,1)S(1)} custom-call(bf16[512,1024]{1,0:T(8,128)(2,1)S(1)} %bitcast.15, s32[1,512]{1,0:T(1,128)S(1)} %bitcast.17, s32[512,1]{1,0:T(8,128)S(1)} %bitcast.14, s32[1,1536]{1,0:T(1,128)S(1)} %bitcast.16, s32[512,1]{1,0:T(8,128)S(1)} %copy.5.row_key_ref, s32[1,1536]{1,0:T(1,128)S(1)} %iota_add_fusion.window_key_ref), custom_call_target="tpu_custom_call" | custom-call | tf_op jit(solution)/shard_map/pallas_call | solution.py:182
  60.0 1.0 %copy.10 = bf16[1,512,1024]{2,1,0:T(8,128)(2,1)} copy(bf16[1,512,1024]{2,1,0:T(8,128)(2,1)S(1)} %bitcast.13) | data formatting | bytes 2097152
  (4 shorter events, 0.0 us)
Async XLA Ops:
  0.0 0.7 %copy-start.2 = (s32[512]{0:T(512)S(1)}, s32[512]{0:T(512)}, u32[]{:S(2)}) copy-start(s32[512]{0:T(512)} %param.4) | copy-start | bytes 6148
  0.8 0.7 %copy-start.1 = (s32[512]{0:T(512)S(1)}, s32[512]{0:T(512)}, u32[]{:S(2)}) copy-start(s32[512]{0:T(512)} %param.5) | copy-start | bytes 6148
  2.0 1.2 %copy-start = (bf16[1,512,1024]{2,1,0:T(8,128)(2,1)S(1)}, bf16[1,512,1024]{2,1,0:T(8,128)(2,1)}, u32[]{:S(2)}) copy-start(bf16[1,512,1024]{2,1,0:T(8,128)(2,1)} %param.3) | copy-start | bytes 3145732

commit v9 on v8

--- a/solution.py
+++ b/solution.py
@@ -23,8 +23,10 @@
     grp = lax.axis_index("grp")
     count = lax.axis_size("wide") * groups
     me = wide * groups + grp
-    left_id = (sec, (me - 1) // groups, (me - 1) % groups)
-    right_id = (sec, (me + 1) // groups, (me + 1) % groups)
+    left = jnp.maximum(me - 1, 0)
+    right = jnp.minimum(me + 1, count - 1)
+    left_id = (sec, left // groups, left % groups)
+    right_id = (sec, right // groups, right % groups)
     return sec, wide, grp, me > 0, me < count - 1, left_id, right_id
 
 

time: 61.2 us -> 61.2 us (level)
  no operation moved by 1% of the time
where the time goes in v9:
time: 61.2 us; the launch traced here: 61 us
  Pallas kernels  56.7 us (93%)
  local copies, waits for them, and re-layouts  4.16 us (7%)
    pallas_call x1, Pallas kernels, exchange(): pl.pallas_call(functools.partial(exchange_kernel, groups), out_shape=jax....  56.7 us
    unnamed x12, local copies, waits for them, and re-layouts  3.86 us

profile of v9, /device:TPU:256, one launch (start us, length us, event | category | flops | bytes accessed | tf_op | source)
XLA Modules:
  0.0 61.0 jit_solution(13328236398603532085)
XLA Ops:
  0.0 0.0 copy-start.2
  0.0 0.7 %copy-done.2 = s32[512]{0:T(512)S(1)} copy-done((s32[512]{0:T(512)S(1)}, s32[512]{0:T(512)}, u32[]{:S(2)}) %copy-start.2) | copy-done | bytes 2072
  0.7 0.1 pad_dynamic-slice_fusion
  0.8 0.1 dynamic_slice.6
  0.8 0.0 copy-start.1
  0.8 0.7 %copy-done.1 = s32[512]{0:T(512)S(1)} copy-done((s32[512]{0:T(512)S(1)}, s32[512]{0:T(512)}, u32[]{:S(2)}) %copy-start.1) | copy-done | bytes 2072
  1.5 0.1 broadcast_bitcast_fusion.1
  1.6 0.1 broadcast_bitcast_fusion
  1.7 0.1 copy.7
  1.8 0.1 copy.5.row_key_ref
  2.0 0.0 copy-start
  2.0 1.2 %copy-done = bf16[1,512,1024]{2,1,0:T(8,128)(2,1)S(1)} copy-done((bf16[1,512,1024]{2,1,0:T(8,128)(2,1)S(1)}, bf16[1,512,1024]{2,1,0:T(8,128)(2,1)}, u32[]{:S(2)}) %copy-start) | copy-done | bytes 1048600
  3.2 56.7 %shard_map.37 = bf16[512,1024]{1,0:T(8,128)(2,1)S(1)} custom-call(bf16[512,1024]{1,0:T(8,128)(2,1)S(1)} %bitcast.15, s32[1,512]{1,0:T(1,128)S(1)} %bitcast.17, s32[512,1]{1,0:T(8,128)S(1)} %bitcast.14, s32[1,1536]{1,0:T(1,128)S(1)} %bitcast.16, s32[512,1]{1,0:T(8,128)S(1)} %copy.5.row_key_ref, s32[1,1536]{1,0:T(1,128)S(1)} %iota_add_fusion.window_key_ref), custom_call_target="tpu_custom_call" | custom-call | tf_op jit(solution)/shard_map/pallas_call | solution.py:184
  60.0 1.0 %copy.10 = bf16[1,512,1024]{2,1,0:T(8,128)(2,1)} copy(bf16[1,512,1024]{2,1,0:T(8,128)(2,1)S(1)} %bitcast.13) | data formatting | bytes 2097152
  (4 shorter events, 0.0 us)
Async XLA Ops:
  0.0 0.7 %copy-start.2 = (s32[512]{0:T(512)S(1)}, s32[512]{0:T(512)}, u32[]{:S(2)}) copy-start(s32[512]{0:T(512)} %param.4) | copy-start | bytes 6148
  0.8 0.7 %copy-start.1 = (s32[512]{0:T(512)S(1)}, s32[512]{0:T(512)}, u32[]{:S(2)}) copy-start(s32[512]{0:T(512)} %param.5) | copy-start | bytes 6148
  2.0 1.2 %copy-start = (bf16[1,512,1024]{2,1,0:T(8,128)(2,1)S(1)}, bf16[1,512,1024]{2,1,0:T(8,128)(2,1)}, u32[]{:S(2)}) copy-start(bf16[1,512,1024]{2,1,0:T(8,128)(2,1)} %param.3) | copy-start | bytes 3145732

commit v10 on v9

--- a/solution.py
+++ b/solution.py
@@ -15,6 +15,7 @@
 MESH_ID = pl.DeviceIdType.MESH
 PIECES = 8
 IN_FLIGHT = 2
+Y_CHIPS = 8
 
 
 def place_of(groups):
@@ -52,6 +53,11 @@
     piece = rows // PIECES
     sec, wide, grp, has_left, has_right, left_id, right_id = place_of(groups)
     partner_id = (1 - sec, wide, grp)
+    me = wide * groups + grp
+    left_cross = has_left & ((me - 1) // groups // Y_CHIPS != wide // Y_CHIPS)
+    right_cross = has_right & ((me + 1) // groups // Y_CHIPS != wide // Y_CHIPS)
+    cross = (left_cross, right_cross)
+    across_id = tuple((1 - sec,) + tuple(peer[1:]) for peer in (left_id, right_id))
 
     pos_win[:, pl.ds(rows, rows)] = pos_ref[...]
     own_copy = pltpu.make_async_copy(own_ref, own_rows, local_sem.at[3])
@@ -76,7 +82,8 @@
             partner_win[place, :] = jnp.zeros((rows, partner_win.shape[1]), partner_win.dtype)
             pos_win[:, pl.ds((1 - d) * 2 * rows, rows)] = jnp.zeros(pos_ref.shape, jnp.int32)
 
-    greet((partner_id,), ((has_left, left_id), (has_right, right_id)))
+    greet((partner_id,), ((has_left, left_id), (has_right, right_id),
+                          (left_cross, across_id[0]), (right_cross, across_id[1])))
 
     def sec_copy(q):
         return pltpu.make_async_remote_copy(
@@ -99,11 +106,23 @@
             send_sem=fwd_send.at[d, q], recv_sem=fwd_recv.at[d, q],
             device_id=left_id if d == 0 else right_id, device_id_type=MESH_ID)
 
+    def cross_copy(d, q):
+        return pltpu.make_async_remote_copy(
+            src_ref=own_ref.at[pl.ds(q * piece, piece)],
+            dst_ref=partner_win.at[pl.ds((1 - d) * 2 * rows + q * piece, piece)],
+            send_sem=fwd_send.at[d, q], recv_sem=fwd_recv.at[d, q],
+            device_id=across_id[d], device_id_type=MESH_ID)
+
     sides = ((0, has_left), (1, has_right))
     for d, present in sides:
         @pl.when(present)
         def _():
             pos_copy(d).start()
+
+        @pl.when(cross[d])
+        def _():
+            for q in range(PIECES):
+                cross_copy(d, q).start()
 
     for q in range(IN_FLIGHT):
         sec_copy(q).start()
@@ -113,7 +132,7 @@
             sec_copy(q + IN_FLIGHT).start()
         sec_copy(q).wait_recv()
         for d, present in sides:
-            @pl.when(present)
+            @pl.when(present & jnp.logical_not(cross[d]))
             def _():
                 fwd_copy(d, q).start()
 
@@ -121,8 +140,16 @@
         @pl.when(present)
         def _():
             pos_copy(d).wait_send()
+
+        @pl.when(present & jnp.logical_not(cross[d]))
+        def _():
             for q in range(PIECES):
                 fwd_copy(d, q).wait_send()
+
+        @pl.when(cross[d])
+        def _():
+            for q in range(PIECES):
+                cross_copy(d, q).wait_send()
 
         arrived = has_right if d == 0 else has_left
 

time: 61.2 us -> 56.6 us (0.925)
  the two profiles are of different devices: /device:TPU:256 before, /device:TPU:251 now
where the time goes in v10:
time: 56.6 us; the launch traced here: 56.4 us
  Pallas kernels  52.2 us (92%)
  local copies, waits for them, and re-layouts  4.16 us (7%)
    pallas_call x1, Pallas kernels, exchange(): pl.pallas_call(functools.partial(exchange_kernel, groups), out_shape=jax....  52.2 us
    unnamed x12, local copies, waits for them, and re-layouts  3.86 us

profile of v10, /device:TPU:251, one launch (start us, length us, event | category | flops | bytes accessed | tf_op | source)
XLA Modules:
  0.0 56.4 jit_solution(12171197042117881298)
XLA Ops:
  0.0 0.0 copy-start.2
  0.0 0.7 %copy-done.2 = s32[512]{0:T(512)S(1)} copy-done((s32[512]{0:T(512)S(1)}, s32[512]{0:T(512)}, u32[]{:S(2)}) %copy-start.2) | copy-done | bytes 2072
  0.7 0.1 pad_dynamic-slice_fusion
  0.8 0.1 dynamic_slice.6
  0.8 0.0 copy-start.1
  0.8 0.7 %copy-done.1 = s32[512]{0:T(512)S(1)} copy-done((s32[512]{0:T(512)S(1)}, s32[512]{0:T(512)}, u32[]{:S(2)}) %copy-start.1) | copy-done | bytes 2072
  1.5 0.1 broadcast_bitcast_fusion.1
  1.6 0.1 broadcast_bitcast_fusion
  1.7 0.1 copy.7
  1.8 0.1 copy.5.row_key_ref
  2.0 0.0 copy-start
  2.0 1.2 %copy-done = bf16[1,512,1024]{2,1,0:T(8,128)(2,1)S(1)} copy-done((bf16[1,512,1024]{2,1,0:T(8,128)(2,1)S(1)}, bf16[1,512,1024]{2,1,0:T(8,128)(2,1)}, u32[]{:S(2)}) %copy-start) | copy-done | bytes 1048600
  3.2 52.2 %shard_map.37 = bf16[512,1024]{1,0:T(8,128)(2,1)S(1)} custom-call(bf16[512,1024]{1,0:T(8,128)(2,1)S(1)} %bitcast.15, s32[1,512]{1,0:T(1,128)S(1)} %bitcast.17, s32[512,1]{1,0:T(8,128)S(1)} %bitcast.14, s32[1,1536]{1,0:T(1,128)S(1)} %bitcast.16, s32[512,1]{1,0:T(8,128)S(1)} %copy.5.row_key_ref, s32[1,1536]{1,0:T(1,128)S(1)} %iota_add_fusion.window_key_ref), custom_call_target="tpu_custom_call" | custom-call | tf_op jit(solution)/shard_map/pallas_call | solution.py:211
  55.4 1.0 %copy.10 = bf16[1,512,1024]{2,1,0:T(8,128)(2,1)} copy(bf16[1,512,1024]{2,1,0:T(8,128)(2,1)S(1)} %bitcast.13) | data formatting | bytes 2097152
  (4 shorter events, 0.0 us)
Async XLA Ops:
  0.0 0.7 %copy-start.2 = (s32[512]{0:T(512)S(1)}, s32[512]{0:T(512)}, u32[]{:S(2)}) copy-start(s32[512]{0:T(512)} %param.4) | copy-start | bytes 6148
  0.8 0.7 %copy-start.1 = (s32[512]{0:T(512)S(1)}, s32[512]{0:T(512)}, u32[]{:S(2)}) copy-start(s32[512]{0:T(512)} %param.5) | copy-start | bytes 6148
  2.0 1.2 %copy-start = (bf16[1,512,1024]{2,1,0:T(8,128)(2,1)S(1)}, bf16[1,512,1024]{2,1,0:T(8,128)(2,1)}, u32[]{:S(2)}) copy-start(bf16[1,512,1024]{2,1,0:T(8,128)(2,1)} %param.3) | copy-start | bytes 3145732

commit v11 on v10

--- a/solution.py
+++ b/solution.py
@@ -16,6 +16,7 @@
 PIECES = 8
 IN_FLIGHT = 2
 Y_CHIPS = 8
+SPLIT = PIECES // 2
 
 
 def place_of(groups):
@@ -121,7 +122,7 @@
 
         @pl.when(cross[d])
         def _():
-            for q in range(PIECES):
+            for q in range(SPLIT):
                 cross_copy(d, q).start()
 
     for q in range(IN_FLIGHT):
@@ -132,7 +133,8 @@
             sec_copy(q + IN_FLIGHT).start()
         sec_copy(q).wait_recv()
         for d, present in sides:
-            @pl.when(present & jnp.logical_not(cross[d]))
+            direct = cross[d] if q < SPLIT else False
+            @pl.when(present & jnp.logical_not(direct))
             def _():
                 fwd_copy(d, q).start()
 
@@ -143,12 +145,17 @@
 
         @pl.when(present & jnp.logical_not(cross[d]))
         def _():
-            for q in range(PIECES):
+            for q in range(SPLIT):
                 fwd_copy(d, q).wait_send()
 
+        @pl.when(present)
+        def _():
+            for q in range(SPLIT, PIECES):
+                fwd_copy(d, q).wait_send()
+
         @pl.when(cross[d])
         def _():
-            for q in range(PIECES):
+            for q in range(SPLIT):
                 cross_copy(d, q).wait_send()
 
         arrived = has_right if d == 0 else has_left

time: 56.6 us -> 59.9 us (1.058)
  the two profiles are of different devices: /device:TPU:251 before, /device:TPU:192 now
where the time goes in v11:
time: 59.9 us; the launch traced here: 59.7 us
  Pallas kernels  55.5 us (93%)
  local copies, waits for them, and re-layouts  4.16 us (7%)
    pallas_call x1, Pallas kernels, exchange(): pl.pallas_call(functools.partial(exchange_kernel, groups), out_shape=jax....  55.5 us
    unnamed x12, local copies, waits for them, and re-layouts  3.86 us

profile of v11, /device:TPU:192, one launch (start us, length us, event | category | flops | bytes accessed | tf_op | source)
XLA Modules:
  0.0 59.7 jit_solution(4708881840347957520)
XLA Ops:
  0.0 0.0 copy-start.2
  0.0 0.7 %copy-done.2 = s32[512]{0:T(512)S(1)} copy-done((s32[512]{0:T(512)S(1)}, s32[512]{0:T(512)}, u32[]{:S(2)}) %copy-start.2) | copy-done | bytes 2072
  0.7 0.1 pad_dynamic-slice_fusion
  0.8 0.1 dynamic_slice.6
  0.8 0.0 copy-start.1
  0.8 0.7 %copy-done.1 = s32[512]{0:T(512)S(1)} copy-done((s32[512]{0:T(512)S(1)}, s32[512]{0:T(512)}, u32[]{:S(2)}) %copy-start.1) | copy-done | bytes 2072
  1.5 0.1 broadcast_bitcast_fusion.1
  1.6 0.1 broadcast_bitcast_fusion
  1.7 0.1 copy.7
  1.8 0.1 copy.5.row_key_ref
  2.0 0.0 copy-start
  2.0 1.2 %copy-done = bf16[1,512,1024]{2,1,0:T(8,128)(2,1)S(1)} copy-done((bf16[1,512,1024]{2,1,0:T(8,128)(2,1)S(1)}, bf16[1,512,1024]{2,1,0:T(8,128)(2,1)}, u32[]{:S(2)}) %copy-start) | copy-done | bytes 1048600
  3.2 55.5 %shard_map.37 = bf16[512,1024]{1,0:T(8,128)(2,1)S(1)} custom-call(bf16[512,1024]{1,0:T(8,128)(2,1)S(1)} %bitcast.15, s32[1,512]{1,0:T(1,128)S(1)} %bitcast.17, s32[512,1]{1,0:T(8,128)S(1)} %bitcast.14, s32[1,1536]{1,0:T(1,128)S(1)} %bitcast.16, s32[512,1]{1,0:T(8,128)S(1)} %copy.5.row_key_ref, s32[1,1536]{1,0:T(1,128)S(1)} %iota_add_fusion.window_key_ref), custom_call_target="tpu_custom_call" | custom-call | tf_op jit(solution)/shard_map/pallas_call | solution.py:218
  58.7 1.0 %copy.10 = bf16[1,512,1024]{2,1,0:T(8,128)(2,1)} copy(bf16[1,512,1024]{2,1,0:T(8,128)(2,1)S(1)} %bitcast.13) | data formatting | bytes 2097152
  (4 shorter events, 0.0 us)
Async XLA Ops:
  0.0 0.7 %copy-start.2 = (s32[512]{0:T(512)S(1)}, s32[512]{0:T(512)}, u32[]{:S(2)}) copy-start(s32[512]{0:T(512)} %param.4) | copy-start | bytes 6148
  0.8 0.7 %copy-start.1 = (s32[512]{0:T(512)S(1)}, s32[512]{0:T(512)}, u32[]{:S(2)}) copy-start(s32[512]{0:T(512)} %param.5) | copy-start | bytes 6148
  2.0 1.2 %copy-start = (bf16[1,512,1024]{2,1,0:T(8,128)(2,1)S(1)}, bf16[1,512,1024]{2,1,0:T(8,128)(2,1)}, u32[]{:S(2)}) copy-start(bf16[1,512,1024]{2,1,0:T(8,128)(2,1)} %param.3) | copy-start | bytes 3145732

commit v12 on v10

--- a/solution.py
+++ b/solution.py
@@ -119,17 +119,20 @@
         def _():
             pos_copy(d).start()
 
-        @pl.when(cross[d])
-        def _():
-            for q in range(PIECES):
+
+    def send_piece(q):
+        sec_copy(q).start()
+        for d in range(2):
+            @pl.when(cross[d])
+            def _():
                 cross_copy(d, q).start()
 
     for q in range(IN_FLIGHT):
-        sec_copy(q).start()
+        send_piece(q)
     for q in range(PIECES):
         sec_copy(q).wait_send()
         if q + IN_FLIGHT < PIECES:
-            sec_copy(q + IN_FLIGHT).start()
+            send_piece(q + IN_FLIGHT)
         sec_copy(q).wait_recv()
         for d, present in sides:
             @pl.when(present & jnp.logical_not(cross[d]))

time: 56.6 us -> 56.6 us (level)
  no operation moved by 1% of the time
where the time goes in v12:
time: 56.6 us; the launch traced here: 56.4 us
  Pallas kernels  52.2 us (92%)
  local copies, waits for them, and re-layouts  4.16 us (7%)
    pallas_call x1, Pallas kernels, exchange(): pl.pallas_call(functools.partial(exchange_kernel, groups), out_shape=jax....  52.2 us
    unnamed x12, local copies, waits for them, and re-layouts  3.86 us

profile of v12, /device:TPU:251, one launch (start us, length us, event | category | flops | bytes accessed | tf_op | source)
XLA Modules:
  0.0 56.4 jit_solution(12050676833748378518)
XLA Ops:
  0.0 0.0 copy-start.2
  0.0 0.7 %copy-done.2 = s32[512]{0:T(512)S(1)} copy-done((s32[512]{0:T(512)S(1)}, s32[512]{0:T(512)}, u32[]{:S(2)}) %copy-start.2) | copy-done | bytes 2072
  0.7 0.1 pad_dynamic-slice_fusion
  0.8 0.1 dynamic_slice.6
  0.8 0.0 copy-start.1
  0.8 0.7 %copy-done.1 = s32[512]{0:T(512)S(1)} copy-done((s32[512]{0:T(512)S(1)}, s32[512]{0:T(512)}, u32[]{:S(2)}) %copy-start.1) | copy-done | bytes 2072
  1.5 0.1 broadcast_bitcast_fusion.1
  1.6 0.1 broadcast_bitcast_fusion
  1.7 0.1 copy.7
  1.8 0.1 copy.5.row_key_ref
  2.0 0.0 copy-start
  2.0 1.2 %copy-done = bf16[1,512,1024]{2,1,0:T(8,128)(2,1)S(1)} copy-done((bf16[1,512,1024]{2,1,0:T(8,128)(2,1)S(1)}, bf16[1,512,1024]{2,1,0:T(8,128)(2,1)}, u32[]{:S(2)}) %copy-start) | copy-done | bytes 1048600
  3.2 52.2 %shard_map.37 = bf16[512,1024]{1,0:T(8,128)(2,1)S(1)} custom-call(bf16[512,1024]{1,0:T(8,128)(2,1)S(1)} %bitcast.15, s32[1,512]{1,0:T(1,128)S(1)} %bitcast.17, s32[512,1]{1,0:T(8,128)S(1)} %bitcast.14, s32[1,1536]{1,0:T(1,128)S(1)} %bitcast.16, s32[512,1]{1,0:T(8,128)S(1)} %copy.5.row_key_ref, s32[1,1536]{1,0:T(1,128)S(1)} %iota_add_fusion.window_key_ref), custom_call_target="tpu_custom_call" | custom-call | tf_op jit(solution)/shard_map/pallas_call | solution.py:214
  55.4 1.0 %copy.10 = bf16[1,512,1024]{2,1,0:T(8,128)(2,1)} copy(bf16[1,512,1024]{2,1,0:T(8,128)(2,1)S(1)} %bitcast.13) | data formatting | bytes 2097152
  (4 shorter events, 0.0 us)
Async XLA Ops:
  0.0 0.7 %copy-start.2 = (s32[512]{0:T(512)S(1)}, s32[512]{0:T(512)}, u32[]{:S(2)}) copy-start(s32[512]{0:T(512)} %param.4) | copy-start | bytes 6148
  0.8 0.7 %copy-start.1 = (s32[512]{0:T(512)S(1)}, s32[512]{0:T(512)}, u32[]{:S(2)}) copy-start(s32[512]{0:T(512)} %param.5) | copy-start | bytes 6148
  2.0 1.2 %copy-start = (bf16[1,512,1024]{2,1,0:T(8,128)(2,1)S(1)}, bf16[1,512,1024]{2,1,0:T(8,128)(2,1)}, u32[]{:S(2)}) copy-start(bf16[1,512,1024]{2,1,0:T(8,128)(2,1)} %param.3) | copy-start | bytes 3145732

commit v13 on v10

--- a/solution.py
+++ b/solution.py
@@ -136,6 +136,23 @@
             def _():
                 fwd_copy(d, q).start()
 
+    own_copy.wait()
+    own_block = own_rows[...]
+
+    def block_scores(k):
+        scores = logit_scale * lax.dot_general(
+            own_block, partner_win[pl.ds(k * rows, rows), :], (((1,), (1,)), ((), ())),
+            preferred_element_type=jnp.float32,
+        )
+        return scores, own_bins_ref[...] == near_bins_ref[:, pl.ds(k * rows, rows)]
+
+    def block_totals(k):
+        scores, allowed = block_scores(k)
+        partial[:, pl.ds(k * rows, rows)] = masked_lse(scores, allowed, 0)
+        return scores, allowed, masked_lse(scores, allowed, 1)
+
+    centre = block_totals(1)
+
     for d, present in sides:
         @pl.when(present)
         def _():
@@ -159,14 +176,11 @@
             for q in range(PIECES):
                 fwd_copy(d, q).wait_recv()
 
-    own_copy.wait()
-    scores = logit_scale * lax.dot_general(
-        own_rows[...], partner_win[...], (((1,), (1,)), ((), ())),
-        preferred_element_type=jnp.float32,
-    )
-    allowed = own_bins_ref[...] == near_bins_ref[...]
-    own_total = masked_lse(scores, allowed, 1)
-    partial[...] = masked_lse(scores, allowed, 0)
+    blocks = (block_totals(0), centre, block_totals(2))
+    row_parts = [b[2] for b in blocks]
+    top = jnp.maximum(jnp.maximum(row_parts[0], row_parts[1]), row_parts[2])
+    top = jnp.where(top > -jnp.inf, top, 0.0)
+    own_total = jnp.log(sum(jnp.exp(p - top) for p in row_parts)) + top
 
     def part_copy(d):
         return pltpu.make_async_remote_copy(
@@ -197,10 +211,15 @@
     partner_total = jnp.log(total) + top
 
     col_key = jnp.where(sec == 0, window_key_ref[...], pos_win[...])
-    hits = allowed & (row_key_ref[...] == col_key)
-    weights = jnp.exp(scores - own_total) + jnp.exp(scores - partner_total)
-    weights = jnp.where(allowed, weights, 0.0) - jnp.where(hits, 2.0, 0.0)
-    grad = jnp.dot(weights.astype(jnp.bfloat16), partner_win[...], preferred_element_type=jnp.float32)
+    grad = None
+    for k, (scores, allowed, _) in enumerate(blocks):
+        columns = slice(k * rows, (k + 1) * rows)
+        hits = allowed & (row_key_ref[...] == col_key[:, columns])
+        weights = jnp.exp(scores - own_total) + jnp.exp(scores - partner_total[:, columns])
+        weights = jnp.where(allowed, weights, 0.0) - jnp.where(hits, 2.0, 0.0)
+        term = jnp.dot(weights.astype(jnp.bfloat16), partner_win[pl.ds(k * rows, rows), :],
+                       preferred_element_type=jnp.float32)
+        grad = term if grad is None else grad + term
     grad_ref[...] = (logit_scale * grad).astype(grad_ref.dtype)
 
 

time: 56.6 us -> 55.8 us (0.986)
  Pallas kernels: 52.2 us -> 51.4 us
    pallas_call x1, Pallas kernels: 52.2 us -> 51.4 us  [exchange(): pl.pallas_call(functools.partial(exchange_kernel, groups), out_shape=jax....]
where the time goes in v13:
time: 55.8 us; the launch traced here: 55.6 us
  Pallas kernels  51.4 us (92%)
  local copies, waits for them, and re-layouts  4.16 us (7%)
    pallas_call x1, Pallas kernels, exchange(): pl.pallas_call(functools.partial(exchange_kernel, groups), out_shape=jax....  51.4 us
    unnamed x12, local copies, waits for them, and re-layouts  3.86 us

profile of v13, /device:TPU:251, one launch (start us, length us, event | category | flops | bytes accessed | tf_op | source)
XLA Modules:
  0.0 55.6 jit_solution(14981252900776641522)
XLA Ops:
  0.0 0.0 copy-start.2
  0.0 0.7 %copy-done.2 = s32[512]{0:T(512)S(1)} copy-done((s32[512]{0:T(512)S(1)}, s32[512]{0:T(512)}, u32[]{:S(2)}) %copy-start.2) | copy-done | bytes 2072
  0.7 0.1 pad_dynamic-slice_fusion
  0.8 0.1 dynamic_slice.6
  0.8 0.0 copy-start.1
  0.8 0.7 %copy-done.1 = s32[512]{0:T(512)S(1)} copy-done((s32[512]{0:T(512)S(1)}, s32[512]{0:T(512)}, u32[]{:S(2)}) %copy-start.1) | copy-done | bytes 2072
  1.5 0.1 broadcast_bitcast_fusion.1
  1.6 0.1 broadcast_bitcast_fusion
  1.7 0.1 copy.7
  1.8 0.1 copy.5.row_key_ref
  2.0 0.0 copy-start
  2.0 1.2 %copy-done = bf16[1,512,1024]{2,1,0:T(8,128)(2,1)S(1)} copy-done((bf16[1,512,1024]{2,1,0:T(8,128)(2,1)S(1)}, bf16[1,512,1024]{2,1,0:T(8,128)(2,1)}, u32[]{:S(2)}) %copy-start) | copy-done | bytes 1048600
  3.2 51.4 %shard_map.37 = bf16[512,1024]{1,0:T(8,128)(2,1)S(1)} custom-call(bf16[512,1024]{1,0:T(8,128)(2,1)S(1)} %bitcast.15, s32[1,512]{1,0:T(1,128)S(1)} %bitcast.17, s32[512,1]{1,0:T(8,128)S(1)} %bitcast.14, s32[1,1536]{1,0:T(1,128)S(1)} %bitcast.16, s32[512,1]{1,0:T(8,128)S(1)} %copy.5.row_key_ref, s32[1,1536]{1,0:T(1,128)S(1)} %iota_add_fusion.window_key_ref), custom_call_target="tpu_custom_call" | custom-call | tf_op jit(solution)/shard_map/pallas_call | solution.py:230
  54.6 1.0 %copy.10 = bf16[1,512,1024]{2,1,0:T(8,128)(2,1)} copy(bf16[1,512,1024]{2,1,0:T(8,128)(2,1)S(1)} %bitcast.13) | data formatting | bytes 2097152
  (4 shorter events, 0.0 us)
Async XLA Ops:
  0.0 0.7 %copy-start.2 = (s32[512]{0:T(512)S(1)}, s32[512]{0:T(512)}, u32[]{:S(2)}) copy-start(s32[512]{0:T(512)} %param.4) | copy-start | bytes 6148
  0.8 0.7 %copy-start.1 = (s32[512]{0:T(512)S(1)}, s32[512]{0:T(512)}, u32[]{:S(2)}) copy-start(s32[512]{0:T(512)} %param.5) | copy-start | bytes 6148
  2.0 1.2 %copy-start = (bf16[1,512,1024]{2,1,0:T(8,128)(2,1)S(1)}, bf16[1,512,1024]{2,1,0:T(8,128)(2,1)}, u32[]{:S(2)}) copy-start(bf16[1,512,1024]{2,1,0:T(8,128)(2,1)} %param.3) | copy-start | bytes 3145732

commit v14 on v13

--- a/solution.py
+++ b/solution.py
@@ -47,8 +47,8 @@
 
 def exchange_kernel(groups, own_ref, pos_ref, own_bins_ref, near_bins_ref, row_key_ref,
                     window_key_ref, grad_ref, partner_win, pos_win, own_rows, partial, held,
-                    local_sem, sec_send, sec_recv, fwd_send, fwd_recv, halo_send, halo_recv,
-                    part_sems):
+                    score_buf, row_buf, local_sem, sec_send, sec_recv, fwd_send, fwd_recv,
+                    halo_send, halo_recv, part_sems):
     rows = own_ref.shape[0]
     piece = rows // PIECES
     sec, wide, grp, has_left, has_right, left_id, right_id = place_of(groups)
@@ -149,26 +149,14 @@
     def block_totals(k):
         scores, allowed = block_scores(k)
         partial[:, pl.ds(k * rows, rows)] = masked_lse(scores, allowed, 0)
-        return scores, allowed, masked_lse(scores, allowed, 1)
-
-    centre = block_totals(1)
-
-    for d, present in sides:
-        @pl.when(present)
-        def _():
-            pos_copy(d).wait_send()
-
-        @pl.when(present & jnp.logical_not(cross[d]))
-        def _():
-            for q in range(PIECES):
-                fwd_copy(d, q).wait_send()
-
-        @pl.when(cross[d])
-        def _():
-            for q in range(PIECES):
-                cross_copy(d, q).wait_send()
-
-        arrived = has_right if d == 0 else has_left
+        score_buf[k] = scores
+        row_buf[k] = masked_lse(scores, allowed, 1)
+
+    block_totals(1)
+
+    def halo_block(k):
+        d = 1 if k == 0 else 0
+        arrived = has_left if k == 0 else has_right
 
         @pl.when(arrived)
         def _():
@@ -176,8 +164,31 @@
             for q in range(PIECES):
                 fwd_copy(d, q).wait_recv()
 
-    blocks = (block_totals(0), centre, block_totals(2))
-    row_parts = [b[2] for b in blocks]
+        block_totals(k)
+
+    for first, second in ((2, 0), (0, 2)):
+        @pl.when((grp == 0) == (first == 2))
+        def _():
+            halo_block(first)
+            halo_block(second)
+
+    for d, present in sides:
+        @pl.when(present)
+        def _():
+            pos_copy(d).wait_send()
+
+        @pl.when(present & jnp.logical_not(cross[d]))
+        def _():
+            for q in range(PIECES):
+                fwd_copy(d, q).wait_send()
+
+        @pl.when(cross[d])
+        def _():
+            for q in range(PIECES):
+                cross_copy(d, q).wait_send()
+
+
+    row_parts = [row_buf[k] for k in range(3)]
     top = jnp.maximum(jnp.maximum(row_parts[0], row_parts[1]), row_parts[2])
     top = jnp.where(top > -jnp.inf, top, 0.0)
     own_total = jnp.log(sum(jnp.exp(p - top) for p in row_parts)) + top
@@ -212,8 +223,10 @@
 
     col_key = jnp.where(sec == 0, window_key_ref[...], pos_win[...])
     grad = None
-    for k, (scores, allowed, _) in enumerate(blocks):
+    for k in range(3):
         columns = slice(k * rows, (k + 1) * rows)
+        scores = score_buf[k]
+        allowed = own_bins_ref[...] == near_bins_ref[:, pl.ds(k * rows, rows)]
         hits = allowed & (row_key_ref[...] == col_key[:, columns])
         weights = jnp.exp(scores - own_total) + jnp.exp(scores - partner_total[:, columns])
         weights = jnp.where(allowed, weights, 0.0) - jnp.where(hits, 2.0, 0.0)
@@ -238,6 +251,8 @@
             pltpu.VMEM((rows, features), own.dtype),
             pltpu.VMEM((1, 3 * rows), jnp.float32),
             pltpu.VMEM((2, 1, 3 * rows), jnp.float32),
+            pltpu.VMEM((3, rows, rows), jnp.float32),
+            pltpu.VMEM((3, rows, 1), jnp.float32),
             pltpu.SemaphoreType.DMA((4,)),
             pltpu.SemaphoreType.DMA((PIECES,)),
             pltpu.SemaphoreType.DMA((PIECES,)),

time: 55.8 us -> 55.6 us (level)
  no operation moved by 1% of the time
where the time goes in v14:
time: 55.6 us; the launch traced here: 55.5 us
  Pallas kernels  51.2 us (92%)
  local copies, waits for them, and re-layouts  4.16 us (7%)
    pallas_call x1, Pallas kernels, exchange(): pl.pallas_call(functools.partial(exchange_kernel, groups), out_shape=jax....  51.2 us
    unnamed x12, local copies, waits for them, and re-layouts  3.86 us

profile of v14, /device:TPU:251, one launch (start us, length us, event | category | flops | bytes accessed | tf_op | source)
XLA Modules:
  0.0 55.5 jit_solution(15034420544563987631)
XLA Ops:
  0.0 0.0 copy-start.2
  0.0 0.7 %copy-done.2 = s32[512]{0:T(512)S(1)} copy-done((s32[512]{0:T(512)S(1)}, s32[512]{0:T(512)}, u32[]{:S(2)}) %copy-start.2) | copy-done | bytes 2072
  0.7 0.1 pad_dynamic-slice_fusion
  0.8 0.1 dynamic_slice.6
  0.8 0.0 copy-start.1
  0.8 0.7 %copy-done.1 = s32[512]{0:T(512)S(1)} copy-done((s32[512]{0:T(512)S(1)}, s32[512]{0:T(512)}, u32[]{:S(2)}) %copy-start.1) | copy-done | bytes 2072
  1.5 0.1 broadcast_bitcast_fusion.1
  1.6 0.1 broadcast_bitcast_fusion
  1.7 0.1 copy.7
  1.8 0.1 copy.5.row_key_ref
  2.0 0.0 copy-start
  2.0 1.2 %copy-done = bf16[1,512,1024]{2,1,0:T(8,128)(2,1)S(1)} copy-done((bf16[1,512,1024]{2,1,0:T(8,128)(2,1)S(1)}, bf16[1,512,1024]{2,1,0:T(8,128)(2,1)}, u32[]{:S(2)}) %copy-start) | copy-done | bytes 1048600
  3.2 51.2 %shard_map.37 = bf16[512,1024]{1,0:T(8,128)(2,1)S(1)} custom-call(bf16[512,1024]{1,0:T(8,128)(2,1)S(1)} %bitcast.15, s32[1,512]{1,0:T(1,128)S(1)} %bitcast.17, s32[512,1]{1,0:T(8,128)S(1)} %bitcast.14, s32[1,1536]{1,0:T(1,128)S(1)} %bitcast.16, s32[512,1]{1,0:T(8,128)S(1)} %copy.5.row_key_ref, s32[1,1536]{1,0:T(1,128)S(1)} %iota_add_fusion.window_key_ref), custom_call_target="tpu_custom_call" | custom-call | tf_op jit(solution)/shard_map/pallas_call | solution.py:243
  54.5 1.0 %copy.10 = bf16[1,512,1024]{2,1,0:T(8,128)(2,1)} copy(bf16[1,512,1024]{2,1,0:T(8,128)(2,1)S(1)} %bitcast.13) | data formatting | bytes 2097152
  (4 shorter events, 0.0 us)
Async XLA Ops:
  0.0 0.7 %copy-start.2 = (s32[512]{0:T(512)S(1)}, s32[512]{0:T(512)}, u32[]{:S(2)}) copy-start(s32[512]{0:T(512)} %param.4) | copy-start | bytes 6148
  0.8 0.7 %copy-start.1 = (s32[512]{0:T(512)S(1)}, s32[512]{0:T(512)}, u32[]{:S(2)}) copy-start(s32[512]{0:T(512)} %param.5) | copy-start | bytes 6148
  2.0 1.2 %copy-start = (bf16[1,512,1024]{2,1,0:T(8,128)(2,1)S(1)}, bf16[1,512,1024]{2,1,0:T(8,128)(2,1)}, u32[]{:S(2)}) copy-start(bf16[1,512,1024]{2,1,0:T(8,128)(2,1)} %param.3) | copy-start | bytes 3145732

commit v15 on v13

--- a/solution.py
+++ b/solution.py
@@ -13,7 +13,7 @@
 
 
 MESH_ID = pl.DeviceIdType.MESH
-PIECES = 8
+PIECES = 4
 IN_FLIGHT = 2
 Y_CHIPS = 8
 
@@ -47,8 +47,8 @@
 
 def exchange_kernel(groups, own_ref, pos_ref, own_bins_ref, near_bins_ref, row_key_ref,
                     window_key_ref, grad_ref, partner_win, pos_win, own_rows, partial, held,
-                    local_sem, sec_send, sec_recv, fwd_send, fwd_recv, halo_send, halo_recv,
-                    part_sems):
+                    centre_buf, local_sem, sec_send, sec_recv, fwd_send, fwd_recv, halo_send,
+                    halo_recv, part_sems):
     rows = own_ref.shape[0]
     piece = rows // PIECES
     sec, wide, grp, has_left, has_right, left_id, right_id = place_of(groups)
@@ -135,8 +135,13 @@
             @pl.when(present & jnp.logical_not(cross[d]))
             def _():
                 fwd_copy(d, q).start()
-
-    own_copy.wait()
+        if q == 0:
+            own_copy.wait()
+        centre_buf[:, pl.ds(q * piece, piece)] = logit_scale * lax.dot_general(
+            own_rows[...], partner_win[pl.ds(rows + q * piece, piece), :],
+            (((1,), (1,)), ((), ())), preferred_element_type=jnp.float32,
+        )
+
     own_block = own_rows[...]
 
     def block_scores(k):
@@ -147,7 +152,11 @@
         return scores, own_bins_ref[...] == near_bins_ref[:, pl.ds(k * rows, rows)]
 
     def block_totals(k):
-        scores, allowed = block_scores(k)
+        if k == 1:
+            scores = centre_buf[...]
+            allowed = own_bins_ref[...] == near_bins_ref[:, pl.ds(rows, rows)]
+        else:
+            scores, allowed = block_scores(k)
         partial[:, pl.ds(k * rows, rows)] = masked_lse(scores, allowed, 0)
         return scores, allowed, masked_lse(scores, allowed, 1)
 
@@ -238,6 +247,7 @@
             pltpu.VMEM((rows, features), own.dtype),
             pltpu.VMEM((1, 3 * rows), jnp.float32),
             pltpu.VMEM((2, 1, 3 * rows), jnp.float32),
+            pltpu.VMEM((rows, rows), jnp.float32),
             pltpu.SemaphoreType.DMA((4,)),
             pltpu.SemaphoreType.DMA((PIECES,)),
             pltpu.SemaphoreType.DMA((PIECES,)),

time: 55.8 us -> 56.1 us (level)
  the two profiles are of different devices: /device:TPU:251 before, /device:TPU:186 now
where the time goes in v15:
time: 56.1 us; the launch traced here: 55.9 us
  Pallas kernels  51.7 us (92%)
  local copies, waits for them, and re-layouts  4.16 us (7%)
    pallas_call x1, Pallas kernels, exchange(): pl.pallas_call(functools.partial(exchange_kernel, groups), out_shape=jax....  51.7 us
    unnamed x12, local copies, waits for them, and re-layouts  3.86 us

profile of v15, /device:TPU:186, one launch (start us, length us, event | category | flops | bytes accessed | tf_op | source)
XLA Modules:
  0.0 55.9 jit_solution(9567241798760961940)
XLA Ops:
  0.0 0.0 copy-start.2
  0.0 0.7 %copy-done.2 = s32[512]{0:T(512)S(1)} copy-done((s32[512]{0:T(512)S(1)}, s32[512]{0:T(512)}, u32[]{:S(2)}) %copy-start.2) | copy-done | bytes 2072
  0.7 0.1 pad_dynamic-slice_fusion
  0.8 0.1 dynamic_slice.6
  0.8 0.0 copy-start.1
  0.8 0.7 %copy-done.1 = s32[512]{0:T(512)S(1)} copy-done((s32[512]{0:T(512)S(1)}, s32[512]{0:T(512)}, u32[]{:S(2)}) %copy-start.1) | copy-done | bytes 2072
  1.5 0.1 broadcast_bitcast_fusion.1
  1.6 0.1 broadcast_bitcast_fusion
  1.7 0.1 copy.7
  1.8 0.1 copy.5.row_key_ref
  2.0 0.0 copy-start
  2.0 1.2 %copy-done = bf16[1,512,1024]{2,1,0:T(8,128)(2,1)S(1)} copy-done((bf16[1,512,1024]{2,1,0:T(8,128)(2,1)S(1)}, bf16[1,512,1024]{2,1,0:T(8,128)(2,1)}, u32[]{:S(2)}) %copy-start) | copy-done | bytes 1048600
  3.2 51.7 %shard_map.37 = bf16[512,1024]{1,0:T(8,128)(2,1)S(1)} custom-call(bf16[512,1024]{1,0:T(8,128)(2,1)S(1)} %bitcast.15, s32[1,512]{1,0:T(1,128)S(1)} %bitcast.17, s32[512,1]{1,0:T(8,128)S(1)} %bitcast.14, s32[1,1536]{1,0:T(1,128)S(1)} %bitcast.16, s32[512,1]{1,0:T(8,128)S(1)} %copy.5.row_key_ref, s32[1,1536]{1,0:T(1,128)S(1)} %iota_add_fusion.window_key_ref), custom_call_target="tpu_custom_call" | custom-call | tf_op jit(solution)/shard_map/pallas_call | solution.py:239
  55.0 1.0 %copy.10 = bf16[1,512,1024]{2,1,0:T(8,128)(2,1)} copy(bf16[1,512,1024]{2,1,0:T(8,128)(2,1)S(1)} %bitcast.13) | data formatting | bytes 2097152
  (4 shorter events, 0.0 us)
Async XLA Ops:
  0.0 0.7 %copy-start.2 = (s32[512]{0:T(512)S(1)}, s32[512]{0:T(512)}, u32[]{:S(2)}) copy-start(s32[512]{0:T(512)} %param.4) | copy-start | bytes 6148
  0.8 0.7 %copy-start.1 = (s32[512]{0:T(512)S(1)}, s32[512]{0:T(512)}, u32[]{:S(2)}) copy-start(s32[512]{0:T(512)} %param.5) | copy-start | bytes 6148
  2.0 1.2 %copy-start = (bf16[1,512,1024]{2,1,0:T(8,128)(2,1)S(1)}, bf16[1,512,1024]{2,1,0:T(8,128)(2,1)}, u32[]{:S(2)}) copy-start(bf16[1,512,1024]{2,1,0:T(8,128)(2,1)} %param.3) | copy-start | bytes 3145732

commit v16 on v13

--- a/solution.py
+++ b/solution.py
@@ -154,20 +154,6 @@
     centre = block_totals(1)
 
     for d, present in sides:
-        @pl.when(present)
-        def _():
-            pos_copy(d).wait_send()
-
-        @pl.when(present & jnp.logical_not(cross[d]))
-        def _():
-            for q in range(PIECES):
-                fwd_copy(d, q).wait_send()
-
-        @pl.when(cross[d])
-        def _():
-            for q in range(PIECES):
-                cross_copy(d, q).wait_send()
-
         arrived = has_right if d == 0 else has_left
 
         @pl.when(arrived)
@@ -221,6 +207,21 @@
                        preferred_element_type=jnp.float32)
         grad = term if grad is None else grad + term
     grad_ref[...] = (logit_scale * grad).astype(grad_ref.dtype)
+
+    for d, present in sides:
+        @pl.when(present)
+        def _():
+            pos_copy(d).wait_send()
+
+        @pl.when(present & jnp.logical_not(cross[d]))
+        def _():
+            for q in range(PIECES):
+                fwd_copy(d, q).wait_send()
+
+        @pl.when(cross[d])
+        def _():
+            for q in range(PIECES):
+                cross_copy(d, q).wait_send()
 
 
 def exchange(own, positives, own_bins, near_bins, row_key, window_key, groups):

time: 55.8 us -> 55.8 us (level)
  no operation moved by 1% of the time
where the time goes in v16:
time: 55.8 us; the launch traced here: 55.6 us
  Pallas kernels  51.4 us (92%)
  local copies, waits for them, and re-layouts  4.16 us (7%)
    pallas_call x1, Pallas kernels, exchange(): pl.pallas_call(functools.partial(exchange_kernel, groups), out_shape=jax....  51.4 us
    unnamed x12, local copies, waits for them, and re-layouts  3.86 us

profile of v16, /device:TPU:251, one launch (start us, length us, event | category | flops | bytes accessed | tf_op | source)
XLA Modules:
  0.0 55.6 jit_solution(2753222721960196480)
XLA Ops:
  0.0 0.0 copy-start.2
  0.0 0.7 %copy-done.2 = s32[512]{0:T(512)S(1)} copy-done((s32[512]{0:T(512)S(1)}, s32[512]{0:T(512)}, u32[]{:S(2)}) %copy-start.2) | copy-done | bytes 2072
  0.7 0.1 pad_dynamic-slice_fusion
  0.8 0.1 dynamic_slice.6
  0.8 0.0 copy-start.1
  0.8 0.7 %copy-done.1 = s32[512]{0:T(512)S(1)} copy-done((s32[512]{0:T(512)S(1)}, s32[512]{0:T(512)}, u32[]{:S(2)}) %copy-start.1) | copy-done | bytes 2072
  1.5 0.1 broadcast_bitcast_fusion.1
  1.6 0.1 broadcast_bitcast_fusion
  1.7 0.1 copy.7
  1.8 0.1 copy.5.row_key_ref
  2.0 0.0 copy-start
  2.0 1.2 %copy-done = bf16[1,512,1024]{2,1,0:T(8,128)(2,1)S(1)} copy-done((bf16[1,512,1024]{2,1,0:T(8,128)(2,1)S(1)}, bf16[1,512,1024]{2,1,0:T(8,128)(2,1)}, u32[]{:S(2)}) %copy-start) | copy-done | bytes 1048600
  3.2 51.4 %shard_map.37 = bf16[512,1024]{1,0:T(8,128)(2,1)S(1)} custom-call(bf16[512,1024]{1,0:T(8,128)(2,1)S(1)} %bitcast.15, s32[1,512]{1,0:T(1,128)S(1)} %bitcast.17, s32[512,1]{1,0:T(8,128)S(1)} %bitcast.14, s32[1,1536]{1,0:T(1,128)S(1)} %bitcast.16, s32[512,1]{1,0:T(8,128)S(1)} %copy.5.row_key_ref, s32[1,1536]{1,0:T(1,128)S(1)} %iota_add_fusion.window_key_ref), custom_call_target="tpu_custom_call" | custom-call | tf_op jit(solution)/shard_map/pallas_call | solution.py:231
  54.6 1.0 %copy.10 = bf16[1,512,1024]{2,1,0:T(8,128)(2,1)} copy(bf16[1,512,1024]{2,1,0:T(8,128)(2,1)S(1)} %bitcast.13) | data formatting | bytes 2097152
  (4 shorter events, 0.0 us)
Async XLA Ops:
  0.0 0.7 %copy-start.2 = (s32[512]{0:T(512)S(1)}, s32[512]{0:T(512)}, u32[]{:S(2)}) copy-start(s32[512]{0:T(512)} %param.4) | copy-start | bytes 6148
  0.8 0.7 %copy-start.1 = (s32[512]{0:T(512)S(1)}, s32[512]{0:T(512)}, u32[]{:S(2)}) copy-start(s32[512]{0:T(512)} %param.5) | copy-start | bytes 6148
  2.0 1.2 %copy-start = (bf16[1,512,1024]{2,1,0:T(8,128)(2,1)S(1)}, bf16[1,512,1024]{2,1,0:T(8,128)(2,1)}, u32[]{:S(2)}) copy-start(bf16[1,512,1024]{2,1,0:T(8,128)(2,1)} %param.3) | copy-start | bytes 3145732

commit v17 on v13

--- a/solution.py
+++ b/solution.py
@@ -119,11 +119,6 @@
         def _():
             pos_copy(d).start()
 
-        @pl.when(cross[d])
-        def _():
-            for q in range(PIECES):
-                cross_copy(d, q).start()
-
     for q in range(IN_FLIGHT):
         sec_copy(q).start()
     for q in range(PIECES):
@@ -135,6 +130,12 @@
             @pl.when(present & jnp.logical_not(cross[d]))
             def _():
                 fwd_copy(d, q).start()
+
+    for d in range(2):
+        @pl.when(cross[d])
+        def _():
+            for q in range(PIECES):
+                cross_copy(d, q).start()
 
     own_copy.wait()
     own_block = own_rows[...]

time: 55.8 us -> 59.2 us (1.061)
  Pallas kernels: 51.4 us -> 54.8 us
    pallas_call x1, Pallas kernels: 51.4 us -> 54.8 us  [exchange(): pl.pallas_call(functools.partial(exchange_kernel, groups), out_shape=jax....]
where the time goes in v17:
time: 59.2 us; the launch traced here: 59 us
  Pallas kernels  54.8 us (93%)
  local copies, waits for them, and re-layouts  4.16 us (7%)
    pallas_call x1, Pallas kernels, exchange(): pl.pallas_call(functools.partial(exchange_kernel, groups), out_shape=jax....  54.8 us
    unnamed x12, local copies, waits for them, and re-layouts  3.86 us

profile of v17, /device:TPU:251, one launch (start us, length us, event | category | flops | bytes accessed | tf_op | source)
XLA Modules:
  0.0 59.0 jit_solution(10863465497778672699)
XLA Ops:
  0.0 0.0 copy-start.2
  0.0 0.7 %copy-done.2 = s32[512]{0:T(512)S(1)} copy-done((s32[512]{0:T(512)S(1)}, s32[512]{0:T(512)}, u32[]{:S(2)}) %copy-start.2) | copy-done | bytes 2072
  0.7 0.1 pad_dynamic-slice_fusion
  0.8 0.1 dynamic_slice.6
  0.8 0.0 copy-start.1
  0.8 0.7 %copy-done.1 = s32[512]{0:T(512)S(1)} copy-done((s32[512]{0:T(512)S(1)}, s32[512]{0:T(512)}, u32[]{:S(2)}) %copy-start.1) | copy-done | bytes 2072
  1.5 0.1 broadcast_bitcast_fusion.1
  1.6 0.1 broadcast_bitcast_fusion
  1.7 0.1 copy.7
  1.8 0.1 copy.5.row_key_ref
  2.0 0.0 copy-start
  2.0 1.2 %copy-done = bf16[1,512,1024]{2,1,0:T(8,128)(2,1)S(1)} copy-done((bf16[1,512,1024]{2,1,0:T(8,128)(2,1)S(1)}, bf16[1,512,1024]{2,1,0:T(8,128)(2,1)}, u32[]{:S(2)}) %copy-start) | copy-done | bytes 1048600
  3.2 54.8 %shard_map.37 = bf16[512,1024]{1,0:T(8,128)(2,1)S(1)} custom-call(bf16[512,1024]{1,0:T(8,128)(2,1)S(1)} %bitcast.15, s32[1,512]{1,0:T(1,128)S(1)} %bitcast.17, s32[512,1]{1,0:T(8,128)S(1)} %bitcast.14, s32[1,1536]{1,0:T(1,128)S(1)} %bitcast.16, s32[512,1]{1,0:T(8,128)S(1)} %copy.5.row_key_ref, s32[1,1536]{1,0:T(1,128)S(1)} %iota_add_fusion.window_key_ref), custom_call_target="tpu_custom_call" | custom-call | tf_op jit(solution)/shard_map/pallas_call | solution.py:231
  58.0 1.0 %copy.10 = bf16[1,512,1024]{2,1,0:T(8,128)(2,1)} copy(bf16[1,512,1024]{2,1,0:T(8,128)(2,1)S(1)} %bitcast.13) | data formatting | bytes 2097152
  (4 shorter events, 0.0 us)
Async XLA Ops:
  0.0 0.7 %copy-start.2 = (s32[512]{0:T(512)S(1)}, s32[512]{0:T(512)}, u32[]{:S(2)}) copy-start(s32[512]{0:T(512)} %param.4) | copy-start | bytes 6148
  0.8 0.7 %copy-start.1 = (s32[512]{0:T(512)S(1)}, s32[512]{0:T(512)}, u32[]{:S(2)}) copy-start(s32[512]{0:T(512)} %param.5) | copy-start | bytes 6148
  2.0 1.2 %copy-start = (bf16[1,512,1024]{2,1,0:T(8,128)(2,1)S(1)}, bf16[1,512,1024]{2,1,0:T(8,128)(2,1)}, u32[]{:S(2)}) copy-start(bf16[1,512,1024]{2,1,0:T(8,128)(2,1)} %param.3) | copy-start | bytes 3145732
